TPU v7x, 256 devices: a whole 4x4x8 slice. The times are simulated.
256 devices in a mesh: gx: 8 (over x_hi, y), gy: 16 (over z, x_lo), af: 2 (over core).
Axes of the slice: x: 4 (x_hi: 2, x_lo: 2; x = x_hi * 2 + x_lo), y: 4, z: 8, core: 2. Of those that a mesh axis runs over, the one named last changes fastest.
Arguments:
- model: float32 [256, 512, 128], P('gx', 'gy'), may hold values from 0.5 to 2
- freq_sq: float32 [4], P('af'), may hold values from 0.5 to 3
- source: float32 [4, 2, 256, 512, 128], P('af', None, 'gx', 'gy'), may hold values from -20 to 20
- observed: float32 [4, 2, 256, 512], P('af', None, 'gx', 'gy'), may hold values from -6 to 6
- receiver_depth: int32 [256, 512], P('gx', 'gy'), may hold values from 0 to 3
Outputs:
- wavefield: float32 [4, 2, 256, 512, 128], P('af', None, 'gx', 'gy')
- gradient: float32 [256, 512, 128], P('gx', 'gy')
Inputs may be any that keep to these rules, and one draw needn't show every extreme that they name: `receiver_depth`: every surface column holds one receiver, at the given depth index.
All inputs are finite; a program needn't handle non-finite values.
Results may differ from a plain program's by a relative error of at most 0.00012.
Values sent between devices are 32-bit elements; how exact they have to be, the bound alone decides.
A program may use at most 64 MiB of HBM per device.

v0:
```python
import jax
import jax.numpy as jnp
from jax import lax
from jax.sharding import PartitionSpec as P

ITERS = 2


attenuation = 0.2
penalty = 4.0


def padded_2(cells, sides, width):
    for axis, dim in sides:
        count = lax.axis_size(axis)
        ends = count - 1
        head = lax.slice_in_dim(cells, 0, width, axis=dim)
        tail = lax.slice_in_dim(cells, cells.shape[dim] - width, cells.shape[dim], axis=dim)
        cells = jnp.concatenate(
            [
                lax.ppermute(tail, axis, [(i, (i + 1) % count) for i in range(ends)]),
                cells,
                lax.ppermute(head, axis, [((i + 1) % count, i) for i in range(ends)]),
            ],
            axis=dim,
        )
    return cells


def stencil_sum(padded):
    center = padded[:, :, 1:-1, 1:-1]
    total = padded[:, :, 2:, 1:-1] + padded[:, :, :-2, 1:-1]
    total = total + padded[:, :, 1:-1, 2:] + padded[:, :, 1:-1, :-2]
    upper = jnp.pad(center[..., 1:], ((0, 0), (0, 0), (0, 0), (0, 0), (0, 1)))
    lower = jnp.pad(center[..., :-1], ((0, 0), (0, 0), (0, 0), (0, 0), (1, 0)))
    return (center, total + upper + lower)


def apply_coef(coef_real, coef_imag, field, sign):
    real_part = coef_real * field[:, 0] - sign * coef_imag * field[:, 1]
    imag_part = coef_real * field[:, 1] + sign * coef_imag * field[:, 0]
    return jnp.stack([real_part, imag_part], axis=1)


def beside(field):
    padded = padded_2(field, (("gx", 2), ("gy", 3)), 1)
    center, total = stencil_sum(padded)
    return total


def inner(left, right):
    return jnp.sum(left * right, axis=(1, 2, 3, 4))


def expand(values):
    return values[:, None, None, None, None]


def on_device(model, freq_sq, source, observed, receiver_depth):
    squared = freq_sq[:, None, None, None]
    coef_real = 6.0 - squared * model[None]
    coef_imag = attenuation * squared * model[None]
    levels = lax.broadcasted_iota(jnp.int32, model.shape, 2)
    onehot = (levels == receiver_depth[:, :, None]).astype(jnp.float32)
    weights = penalty * onehot

    def forward(field):
        return apply_coef(coef_real, coef_imag, field, 1.0) - beside(field)

    def adjoint(field):
        return apply_coef(coef_real, coef_imag, field, -1.0) - beside(field)

    rhs = adjoint(source) + weights * observed[:, :, :, :, None]
    field = jnp.zeros_like(rhs)
    resid = rhs

    def squares(values):
        return lax.psum(inner(values, values), ("gx", "gy"))

    direction = rhs
    norm_now = squares(resid)
    for sweep in range(ITERS):
        image = adjoint(forward(direction)) + weights * direction
        alpha = norm_now / lax.psum(inner(direction, image), ("gx", "gy"))
        field = field + expand(alpha) * direction
        resid = resid - expand(alpha) * image
        norm_next = squares(resid)
        direction = resid + expand(norm_next / norm_now) * direction
        norm_now = norm_next
    misfit = forward(field) - source
    deriv_real = -squared
    deriv_imag = attenuation * squared
    wave_real = deriv_real * field[:, 0] - deriv_imag * field[:, 1]
    wave_imag = deriv_real * field[:, 1] + deriv_imag * field[:, 0]
    local_terms = jnp.sum(wave_real * misfit[:, 0] + wave_imag * misfit[:, 1], axis=0)
    gradient = lax.psum(local_terms, "af")
    return (field, gradient)


def solution(mesh):
    in_specs = (
        P("gx", "gy", None),
        P("af"),
        P("af", None, "gx", "gy", None),
        P("af", None, "gx", "gy"),
        P("gx", "gy"),
    )
    out_specs = (P("af", None, "gx", "gy", None), P("gx", "gy", None))
    return jax.shard_map(
        on_device, mesh=mesh, in_specs=in_specs, out_specs=out_specs, check_vma=False
    )
```

profile of v0, /device:TPU:1, one launch (start us, length us, event | category | flops | bytes accessed | tf_op | source)
XLA Modules:
  0.0 1227.7 jit_solution(6360724979951832859)
XLA Ops:
  7.2 0.9 fusion.80
  8.2 1.3 collective-permute-start
  9.6 4.8 collective-permute-start.1
  14.4 2.8 copy.48
  17.5 2.8 fusion.79
  20.3 1.8 fusion.48
  22.2 0.7 pad_maximum_fusion.62
  22.9 1.3 collective-permute-start.2
  24.2 4.0 collective-permute-start.3
  28.4 0.9 copy.58
  29.4 1.4 collective-permute-done.3
  30.8 7.4 fusion.45
  38.3 1.3 collective-permute-start.4
  39.6 4.0 collective-permute-start.5
  43.6 0.8 fusion.77
  44.4 0.5 collective-permute-done.5
  44.9 1.3 collective-permute-start.6
  46.2 4.3 collective-permute-start.7
  51.0 1.1 collective-permute-done.7
  52.0 2.1 fusion.38
  54.3 1.3 collective-permute-start.8
  55.6 4.6 collective-permute-start.9
  60.2 0.7 fusion.76
  61.0 0.5 collective-permute-done.9
  61.5 1.3 collective-permute-start.10
  62.8 4.9 collective-permute-start.11
  67.7 0.4 fusion.50
  68.2 1.1 collective-permute-done.11
  69.3 4.1 multiply_reduce_fusion.1
  73.4 305.5 %all-reduce.12 = (f32[2]{0:T(128)S(1)}, f32[2]{0:T(128)S(1)}) all-reduce(f32[2]{0:T(128)S(1)} %get-tuple-element.7, f32[2]{0:T(128)S(1)} %get-tuple-element.6), channel_id=1, replica_groups=mesh['gx'=8,'gy'=16,'af'=2] {'gx','gy'}, use_global_device_ids=true, to_apply=%region_1.2 | all-reduce | flops 4 | bytes 32 | tf_op jit(solution)/shard_map/psum | solution.py:78
  378.9 2.1 multiply_reduce_fusion
  381.0 286.8 %psum.37 = f32[2]{0:T(128)S(1)} all-reduce(f32[2]{0:T(128)S(1)} %multiply_reduce_fusion), channel_id=1, replica_groups=mesh['gx'=8,'gy'=16,'af'=2] {'gx','gy'}, use_global_device_ids=true, to_apply=%region_5.6 | all-reduce | flops 2 | bytes 16 | tf_op jit(solution)/shard_map/psum | solution.py:78
  667.8 2.2 multiply_add_fusion.1
  670.1 1.3 collective-permute-start.12
  671.4 4.2 collective-permute-start.13
  675.5 0.7 fusion.73
  676.7 1.3 collective-permute-start.14
  678.0 4.1 collective-permute-start.15
  682.5 1.1 collective-permute-done.15
  683.6 2.0 fusion.25
  685.7 1.3 collective-permute-start.16
  687.0 4.3 collective-permute-start.17
  691.3 0.7 fusion.71
  692.1 0.5 collective-permute-done.17
  692.7 1.3 collective-permute-start.18
  694.0 4.9 collective-permute-start.19
  698.9 0.4 fusion.52
  699.3 1.5 collective-permute-done.19
  700.8 3.0 fusion.19
  703.8 289.7 %psum.38 = f32[2]{0:T(128)S(1)} all-reduce(f32[2]{0:T(128)S(1)} %fusion.19), channel_id=1, replica_groups=mesh['gx'=8,'gy'=16,'af'=2] {'gx','gy'}, use_global_device_ids=true, to_apply=%region_7.8 | all-reduce | flops 2 | bytes 16 | tf_op jit(solution)/shard_map/psum | solution.py:84
  993.6 2.2 multiply_add_fusion
  995.8 0.4 fusion.58
  996.3 0.7 fusion.69
  997.0 1.3 collective-permute-start.20
  998.3 4.0 collective-permute-start.21
  1002.5 1.1 collective-permute-done.21
  1003.6 1.3 collective-permute-start.22
  1005.0 4.1 collective-permute-start.23
  1009.5 1.1 collective-permute-done.23
  1010.6 2.7 fusion.10
  1013.2 1.4 fusion.62
  1014.7 4.1 copy.70
  1018.8 199.9 %all-reduce.15.cloned.1.call-done = f32[32,32,128]{2,0,1:T(8,128)} async-done(((f32[32,32,128]{2,0,1:T(8,128)}), f32[32,32,128]{2,0,1:T(8,128)}) %all-reduce.15.cloned.1.call-update) | async-done | bytes 524304 | tf_op jit(solution)/shard_map/psum | solution.py:96
  1218.7 2.1 copy.71
  (53 shorter events, 3.2 us)
Async XLA Ops:
  7.2 1211.5 %all-reduce.15.cloned.1.call-start = ((), (), s32[]{:S(2)}) async-start(), calls=%async_computation | async-start | bytes 1048576 | tf_op jit(solution)/shard_map/psum | solution.py:96
  8.2 14.1 %collective-permute-start = (f32[2,2,1,32,128]{4,2,3,0,1:T(1,128)S(1)}, f32[2,2,1,32,128]{4,2,3,0,1:T(1,128)S(1)}, u32[]{:S(2)}, u32[]{:S(2)}) collective-permute-start(f32[2,2,1,32,128]{4,2,3,0,1:T(1,128)S(1)} %copy.50), channel_id=1, source_target_pairs={{32,0},{64,32},{96,64},{128,96},{160,128},{192,160},{224,192},{33,... | collective-permute-start | bytes 196616 | tf_op jit(solution)/shard_map/ppermute | solution.py:23
  9.6 7.6 copy-start.5
  9.6 7.6 copy-start.4
  9.6 12.7 %collective-permute-start.1 = (f32[2,2,1,32,128]{4,2,3,0,1:T(1,128)S(1)}, f32[2,2,1,32,128]{4,2,3,0,1:T(1,128)S(1)}, u32[]{:S(2)}, u32[]{:S(2)}) collective-permute-start(f32[2,2,1,32,128]{4,2,3,0,1:T(1,128)S(1)} %copy.52), channel_id=1, source_target_pairs={{0,32},{32,64},{64,96},{96,128},{128,160},{160,192},{192,224},{1,3... | collective-permute-start | bytes 196616 | tf_op jit(solution)/shard_map/ppermute | solution.py:21
  17.2 5.0 copy-start.2
  20.3 1.8 copy-start.6
  22.9 6.4 collective-permute-start.2
  24.2 6.6 collective-permute-start.3
  38.3 6.1 collective-permute-start.4
  39.6 5.3 collective-permute-start.5
  44.9 6.0 collective-permute-start.6
  46.2 5.8 collective-permute-start.7
  54.3 6.7 collective-permute-start.8
  55.6 5.9 collective-permute-start.9
  61.5 6.6 collective-permute-start.10
  62.8 6.5 collective-permute-start.11
  670.0 30.9 %copy-start.1 = (f32[2,2,32,32,128]{4,2,3,0,1:T(8,128)}, f32[2,2,32,32,128]{4,2,3,0,1:T(8,128)S(1)}, u32[]{:S(2)}) copy-start(f32[2,2,32,32,128]{4,2,3,0,1:T(8,128)S(1)} %multiply_add_fusion.1) | copy-start | bytes 6291460
  670.1 6.2 collective-permute-start.12
  671.4 5.3 collective-permute-start.13
  676.7 5.8 collective-permute-start.14
  678.0 5.6 collective-permute-start.15
  685.7 6.4 collective-permute-start.16
  687.0 5.6 collective-permute-start.17
  692.7 6.6 collective-permute-start.18
  694.0 6.8 collective-permute-start.19
  995.7 17.5 %copy-start = (f32[2,2,32,32,128]{4,2,3,0,1:T(8,128)}, f32[2,2,32,32,128]{4,2,3,0,1:T(8,128)S(1)}, u32[]{:S(2)}) copy-start(f32[2,2,32,32,128]{4,2,3,0,1:T(8,128)S(1)} %multiply_add_fusion) | copy-start | bytes 6291460
  997.0 5.5 collective-permute-start.20
  998.3 5.3 collective-permute-start.21
  1003.6 5.8 collective-permute-start.22
  1004.9 5.6 copy-start.3
  1005.0 5.6 collective-permute-start.23
Sparse Core Ops, SparseCore 0:
  1014.8 203.8 all-reduce.14
where the time goes:
time: 1230 us
  blocking collectives  882 us (72%)
  waiting for transfers between devices  210 us (17%)
  starting transfers between devices  67.7 us (6%)
  other arithmetic  34.7 us (3%)
  local copies, waits for them, and re-layouts  18.4 us (1%)
  between operations  14.6 us (1%)
    psum x2, blocking collectives, squares(): return lax.psum(inner(values, values), ('gx', 'gy'))  592 us
    psum x1, blocking collectives, on_device(): alpha = norm_now / lax.psum(inner(direction, image), ('gx', 'gy'))  290 us
    psum x1, waiting for transfers between devices, on_device(): gradient = lax.psum(local_terms, 'af')  200 us
    ppermute x12, starting transfers between devices, padded_2(): lax.ppermute(tail, axis, [(i, (i + 1) % count) for i in range(ends)])  52.2 us
  transfers between devices with their start and end apart: 25, of which 12 were waited for; matrix products, arithmetic and copies ran while one was open for 1% of the time, Pallas kernels for 0%

commit v1 on v0

v1 whole, which is shorter than its diff:
```python
import functools

import jax
import jax.numpy as jnp
from jax import lax
from jax.experimental import pallas as pl
from jax.experimental.pallas import tpu as pltpu
from jax.sharding import PartitionSpec as P

MESH = pl.DeviceIdType.MESH
ATTENUATION = 0.2
PENALTY = 4.0
PAD = 8


def kernel(dims, model_h, fsq, src_h, obs_h, depth_h, field_o, grad_o,
           S, B, U, Q, PP, M, W, WO, OB, DP, HX, HY, YS, A1S, A1R, A2S, A2R, GS, GR,
           load_sem, hs_sem, hr_sem, a1s_sem, a1r_sem, a2s_sem, a2r_sem, gs_sem, gr_sem):
    GX, GY, XL, YL, NGC = dims
    PX, PY = XL + 2, YL + 2 * PAD
    NT = YL // 8
    XT = XL // 8
    N1 = GX * 2
    N2 = GY // 2
    gx = lax.axis_index("gx")
    gy = lax.axis_index("gy")
    af = lax.axis_index("af")

    loads = [
        pltpu.make_async_copy(depth_h, DP, load_sem.at[XL]),
        pltpu.make_async_copy(obs_h, OB, load_sem.at[XL + 1]),
        pltpu.make_async_copy(model_h, M, load_sem.at[XL + 2]),
    ] + [
        pltpu.make_async_copy(src_h.at[:, x], S.at[:, pl.ds((1 + x) * PY + PAD, YL), :], load_sem.at[x])
        for x in range(XL)
    ]
    for cp in loads:
        cp.start()

    def first(j):
        r = lax.rem(gx * 2 + lax.rem(gy, 2) + j, N1)
        return r // 2, (gy // 2) * 2 + lax.rem(r, 2)

    def second(j):
        return lax.rem(gy // 2 + j, N2) * 2 + lax.rem(gy, 2)

    barrier = pltpu.get_barrier_semaphore()
    for j in range(1, N1):
        px, py = first(j)
        pl.semaphore_signal(barrier, inc=1, device_id={"gx": px, "gy": py}, device_id_type=MESH)
    for j in range(1, N2):
        pl.semaphore_signal(barrier, inc=1, device_id={"gy": second(j)}, device_id_type=MESH)
    pl.semaphore_signal(barrier, inc=1, device_id={"af": 1 - af}, device_id_type=MESH)

    @pl.when(gy > 0)
    def _():
        pl.semaphore_signal(barrier, inc=1, device_id={"gy": gy - 1}, device_id_type=MESH)

    @pl.when(gy < GY - 1)
    def _():
        pl.semaphore_signal(barrier, inc=1, device_id={"gy": gy + 1}, device_id_type=MESH)

    zero = jnp.zeros((8, 128), jnp.float32)

    def clear_rows(x, _):
        o = pl.multiple_of(x * PY, 8)
        for ref in (S, B, U, Q):
            for c in range(4):
                ref[c, pl.ds(o, 8), :] = zero
                ref[c, pl.ds(o + PAD + YL, 8), :] = zero
        return 0

    lax.fori_loop(0, PX, clear_rows, 0)
    for ref in (S, B, U, Q):
        for c in range(4):
            for xx in (0, PX - 1):
                for t in range(NT):
                    ref[c, pl.ds(xx * PY + PAD + t * 8, 8), :] = zero

    for k in range(2):
        A1S[k] = zero

    def clear_halo(ref, side, count):
        for e in range(4):
            for c in range(4):
                for r in range(0, count, 8):
                    ref[e, side, c, pl.ds(r, 8), :] = zero

    for cond, ref, side, count in ((gx == 0, HX, 0, YL), (gx == GX - 1, HX, 1, YL),
                                   (gy == 0, HY, 0, XL), (gy == GY - 1, HY, 1, XL)):
        pl.when(cond)(functools.partial(clear_halo, ref, side, count))

    def copies(e, V):
        out = []
        plan = (
            (gy > 0, {"gy": gy - 1}, YS.at[e, 0], HY.at[e, 1], 2, 3),
            (gy < GY - 1, {"gy": gy + 1}, YS.at[e, 1], HY.at[e, 0], 3, 2),
            (gx > 0, {"gx": gx - 1}, V.at[:, pl.ds(PY + PAD, YL), :],
             HX.at[e, 1], 0, 1),
            (gx < GX - 1, {"gx": gx + 1}, V.at[:, pl.ds(XL * PY + PAD, YL), :],
             HX.at[e, 0], 1, 0),
        )
        for cond, dev, s, d, mine, theirs in plan:
            out.append((cond, pltpu.make_async_remote_copy(
                src_ref=s, dst_ref=d, send_sem=hs_sem.at[e, mine], recv_sem=hr_sem.at[e, theirs],
                device_id=dev, device_id_type=MESH)))
        return out

    def send(e, V):
        for side, yy in ((0, PAD), (1, PAD + YL - 1)):
            for c in range(4):
                for k in range(XT):
                    YS[e, side, c, pl.ds(k * 8, 8), :] = V[c, pl.ds((1 + 8 * k) * PY + yy, 8, stride=PY), :]
        for cond, cp in copies(e, V):
            pl.when(cond)(cp.start)

    def arrive(e, V):
        cps = copies(e, V)
        for (cond, _), (_, cp) in zip(cps, (cps[1], cps[0], cps[3], cps[2])):
            pl.when(cond)(cp.wait_recv)

    def drain(e, V):
        for cond, cp in copies(e, V):
            pl.when(cond)(cp.wait_send)

    lane = lax.broadcasted_iota(jnp.int32, (8, 128), 1)
    at_first = lane == 0
    at_last = lane == 127
    sq = [fsq[0], fsq[1]]

    def around(V, c, o):
        cen = V[c, pl.ds(o, 8), :]
        t = V[c, pl.ds(o - PY, 8), :] + V[c, pl.ds(o + PY, 8), :]
        t = t + (V[c, pl.ds(o - 1, 8), :] + V[c, pl.ds(o + 1, 8), :])
        lo = jnp.where(at_first, 0.0, pltpu.roll(cen, 1, 1))
        hi = jnp.where(at_last, 0.0, pltpu.roll(cen, 127, 1))
        return cen, t + (lo + hi)

    def sweep(V, sign, finish, carry):
        def body(x, carry):
            o0 = pl.multiple_of(x * PY, 8)
            r0 = pl.multiple_of(x * YL, 8)
            for t in range(NT):
                m = M[pl.ds(r0 + t * 8, 8), :]
                for f in range(2):
                    k = sq[f] * m
                    cr = 6.0 - k
                    ci = (sign * ATTENUATION) * k
                    o = o0 + PY + PAD + t * 8
                    re, nre = around(V, 2 * f, o)
                    im, nim = around(V, 2 * f + 1, o)
                    out = (cr * re - ci * im - nre, cr * im + ci * re - nim)
                    carry = finish(f, o, r0 + t * 8, (re, im), out, carry)
            return carry
        return lax.fori_loop(0, XL, body, carry)

    def correct(e, rows, step, carry):
        for side in range(2):
            for c in range(4):
                for t in range(NT):
                    idx = rows(c, 1 + side * (XL - 1), PAD + t * 8, False)
                    carry = step(c // 2, idx, HX[e, side, c, pl.ds(t * 8, 8), :], carry)
        for side in range(2):
            for c in range(4):
                for k in range(XT):
                    idx = rows(c, 1 + 8 * k, PAD + side * (YL - 1), True)
                    carry = step(c // 2, idx, HY[e, side, c, pl.ds(k * 8, 8), :], carry)
        return carry

    def padded(c, xx, yy, strided):
        o = xx * PY + yy
        return c, pl.ds(o, 8, stride=PY) if strided else pl.ds(o, 8)

    def compact(c, xx, yy, strided):
        o = (xx - 1) * YL + yy - PAD
        return c, pl.ds(o, 8, stride=YL) if strided else pl.ds(o, 8)

    loads[0].wait()
    loads[1].wait()
    dt = jnp.transpose(jnp.concatenate(
        [DP[...].astype(jnp.float32), jnp.zeros((XL, 128 - YL), jnp.float32)], axis=1))
    ot = jnp.transpose(jnp.concatenate(
        [OB[...], jnp.zeros((4 * XL, 128 - YL), jnp.float32)], axis=1))
    lanef = lane.astype(jnp.float32)
    for x in range(XL):
        for t in range(NT):
            d = jnp.broadcast_to(dt[t * 8:t * 8 + 8, x:x + 1], (8, 128))
            w = jnp.where(lanef == d, PENALTY, 0.0)
            W[pl.ds(x * YL + t * 8, 8), :] = w
            for c in range(4):
                ob = jnp.broadcast_to(ot[t * 8:t * 8 + 8, c * XL + x:c * XL + x + 1], (8, 128))
                WO[c, pl.ds(x * YL + t * 8, 8), :] = w * ob

    for cp in loads[2:]:
        cp.wait()
    pl.semaphore_wait(barrier, N1 - 1 + N2 - 1 + 1 + (gy > 0).astype(jnp.int32) + (gy < GY - 1).astype(jnp.int32))
    send(0, S)

    def finish_b(f, o, r, cen, out, carry):
        acc = carry[f]
        for c in range(2):
            v = out[c] + WO[2 * f + c, pl.ds(r, 8), :]
            B[2 * f + c, pl.ds(o, 8), :] = v
            acc = acc + v * v
        return tuple(acc if i == f else carry[i] for i in range(2))

    def fix_field(ref, rows_of):
        def step(f, idx, h, carry):
            old = ref[idx[0], idx[1], :]
            new = old - h
            ref[idx[0], idx[1], :] = new
            d = h * (h - 2.0 * old)
            return tuple(carry[i] + d if i == f else carry[i] for i in range(2))
        return step

    rr = sweep(S, -1.0, finish_b, (zero, zero))
    arrive(0, S)
    rr = correct(0, padded, fix_field(B, padded), rr)
    send(1, B)

    def finish_u(f, o, r, cen, out, carry):
        acc = carry[f]
        for c in range(2):
            U[2 * f + c, pl.ds(o, 8), :] = out[c]
            acc = acc + out[c] * out[c]
        return tuple(acc if i == f else carry[i] for i in range(2))

    dq = sweep(B, 1.0, finish_u, (zero, zero))
    arrive(1, B)
    dq = correct(1, padded, fix_field(U, padded), dq)
    send(2, U)

    def finish_q(f, o, r, cen, out, carry):
        acc = carry[f]
        w = W[pl.ds(r, 8), :]
        for c in range(2):
            b = B[2 * f + c, pl.ds(o, 8), :]
            wb = w * b
            Q[2 * f + c, pl.ds(o, 8), :] = out[c] + wb
            acc = acc + wb * b
        return tuple(acc if i == f else carry[i] for i in range(2))

    dq = sweep(U, -1.0, finish_q, dq)

    def reduce_first(k, parts):
        for i, v in enumerate(parts):
            A1S[k, pl.ds(i, 1), :] = jnp.sum(v, axis=0, keepdims=True)
        for j in range(1, N1):
            px, py = first(j)
            pltpu.make_async_remote_copy(
                src_ref=A1S.at[k], dst_ref=A1R.at[k, N1 - j], send_sem=a1s_sem.at[k, j], recv_sem=a1r_sem.at[k, N1 - j],
                device_id={"gx": px, "gy": py}, device_id_type=MESH).start()

    def first_copy(k, j):
        px, py = first(j)
        return pltpu.make_async_remote_copy(
            src_ref=A1S.at[k], dst_ref=A1R.at[k, j], send_sem=a1s_sem.at[k, j], recv_sem=a1r_sem.at[k, j],
            device_id={"gx": px, "gy": py}, device_id_type=MESH)

    def second_copy(k, j, slot):
        return pltpu.make_async_remote_copy(
            src_ref=A2S.at[k], dst_ref=A2R.at[k, slot], send_sem=a2s_sem.at[k, j], recv_sem=a2r_sem.at[k, slot],
            device_id={"gy": second(j)}, device_id_type=MESH)

    def reduce_second(k):
        total = A1S[k]
        for j in range(1, N1):
            first_copy(k, j).wait_recv()
        for j in range(1, N1):
            total = total + A1R[k, j]
        A2S[k] = total
        for j in range(1, N2):
            second_copy(k, j, N2 - j).start()

    def reduce_end(k):
        total = A2S[k]
        for j in range(1, N2):
            second_copy(k, j, j).wait_recv()
        for j in range(1, N2):
            total = total + A2R[k, j]
        return jnp.broadcast_to(jnp.sum(total, axis=1, keepdims=True), (8, 128))

    def row(tile, i):
        return jnp.broadcast_to(tile[i:i + 1, :], (8, 128))

    reduce_first(0, (rr[0], rr[1], dq[0], dq[1]))

    arrive(2, U)

    def fix_plain(ref):
        def step(f, idx, h, carry):
            ref[idx[0], idx[1], :] = ref[idx[0], idx[1], :] - h
            return carry
        return step

    correct(2, padded, fix_plain(Q), 0)
    send(3, Q)
    reduce_second(0)

    def finish_p(f, o, r, cen, out, carry):
        for c in range(2):
            PP[2 * f + c, pl.ds(r, 8), :] = out[c]
        return carry

    sweep(Q, 1.0, finish_p, 0)
    sums = reduce_end(0)
    norm0 = [row(sums, f) for f in range(2)]
    curv0 = [row(sums, 2 + f) for f in range(2)]
    alpha0 = [norm0[f] / curv0[f] for f in range(2)]
    arrive(3, Q)
    correct(3, compact, fix_plain(PP), 0)

    def tally(x, carry):
        o0 = pl.multiple_of(x * PY, 8)
        r0 = pl.multiple_of(x * YL, 8)
        carry = list(carry)
        for t in range(NT):
            w = W[pl.ds(r0 + t * 8, 8), :]
            for f in range(2):
                for c in range(2):
                    off = PY + PAD + t * 8
                    q = Q[2 * f + c, pl.ds(o0 + off, 8), :]
                    r1 = B[2 * f + c, pl.ds(o0 + off, 8), :] - alpha0[f] * q
                    ar = U[2 * f + c, pl.ds(o0 + off, 8), :] - alpha0[f] * PP[2 * f + c, pl.ds(r0 + t * 8, 8), :]
                    r2 = r1 * r1
                    carry[f] = carry[f] + r2
                    carry[2 + f] = carry[2 + f] + (ar * ar + w * r2)
                    carry[4 + f] = carry[4 + f] + r1 * q
        return tuple(carry)

    tallies = lax.fori_loop(0, XL, tally, (zero,) * 6)
    reduce_first(1, tallies)
    reduce_second(1)
    sums = reduce_end(1)

    cb, cq = [], []
    for f in range(2):
        norm1 = row(sums, f)
        beta = norm1 / norm0[f]
        curv1 = row(sums, 2 + f) + (2.0 * beta) * row(sums, 4 + f) + (beta * beta) * curv0[f]
        alpha1 = norm1 / curv1
        cb.append(alpha0[f] + alpha1 * (1.0 + beta))
        cq.append(-(alpha0[f] * alpha1))

    GROWS = XL * YL // NGC
    def grad_copy(g):
        return pltpu.make_async_remote_copy(
            src_ref=GS.at[pl.ds(g * GROWS, GROWS), :], dst_ref=GR.at[pl.ds(g * GROWS, GROWS), :],
            send_sem=gs_sem.at[g], recv_sem=gr_sem.at[g], device_id={"af": 1 - af}, device_id_type=MESH)

    def outputs(x, _):
        o0 = pl.multiple_of(x * PY, 8)
        r0 = pl.multiple_of(x * YL, 8)
        for t in range(NT):
            g = zero
            for f in range(2):
                fld, mis = [], []
                for c in range(2):
                    off = PY + PAD + t * 8
                    ro = (2 * f + c) * XL * YL + r0 + t * 8
                    v = cb[f] * B[2 * f + c, pl.ds(o0 + off, 8), :] + cq[f] * Q[2 * f + c, pl.ds(o0 + off, 8), :]
                    field_o[pl.ds(ro, 8), :] = v
                    fld.append(v)
                    mis.append(cb[f] * U[2 * f + c, pl.ds(o0 + off, 8), :] + cq[f] * PP[2 * f + c, pl.ds(r0 + t * 8, 8), :] - S[2 * f + c, pl.ds(o0 + off, 8), :])
                wr = -fld[0] - ATTENUATION * fld[1]
                wi = ATTENUATION * fld[0] - fld[1]
                g = g + sq[f] * (wr * mis[0] + wi * mis[1])
            GS[pl.ds(r0 + t * 8, 8), :] = g
        return 0

    for g in range(NGC):
        lax.fori_loop(g * (XL // NGC), (g + 1) * (XL // NGC), outputs, 0)
        grad_copy(g).start()

    for g in range(NGC):
        grad_copy(g).wait_recv()

        def add(i, _):
            o = pl.multiple_of(i * 8, 8)
            grad_o[pl.ds(o, 8), :] = GS[pl.ds(o, 8), :] + GR[pl.ds(o, 8), :]
            return 0

        lax.fori_loop(g * GROWS // 8, (g + 1) * GROWS // 8, add, 0)

    for g in range(NGC):
        grad_copy(g).wait_send()
    for e, V in enumerate((S, B, U, Q)):
        drain(e, V)
    for k in range(2):
        for j in range(1, N1):
            first_copy(k, j).wait_send()
        for j in range(1, N2):
            second_copy(k, j, j).wait_send()


def solution(mesh):
    GX, GY = mesh.shape["gx"], mesh.shape["gy"]

    def on_device(model, freq_sq, source, observed, receiver_depth):
        XL, YL, ZL = model.shape
        PX, PY = XL + 2, YL + 2 * PAD
        f32 = jnp.float32
        N1, N2 = GX * 2, GY // 2
        NGC = 4
        big = pltpu.VMEM((4, PX * PY, ZL), f32)
        col = pltpu.VMEM((XL * YL, ZL), f32)
        dma = pltpu.SemaphoreType.DMA
        field, grad = pl.pallas_call(
            functools.partial(kernel, (GX, GY, XL, YL, NGC)),
            out_shape=(jax.ShapeDtypeStruct((4 * XL * YL, ZL), f32),
                       jax.ShapeDtypeStruct((XL * YL, ZL), f32)),
            in_specs=[pl.BlockSpec(memory_space=pl.ANY),
                      pl.BlockSpec(memory_space=pltpu.SMEM),
                      pl.BlockSpec(memory_space=pl.ANY),
                      pl.BlockSpec(memory_space=pl.ANY),
                      pl.BlockSpec(memory_space=pl.ANY)],
            out_specs=(pl.BlockSpec(memory_space=pltpu.VMEM),) * 2,
            scratch_shapes=[
                big, big, big, big,
                pltpu.VMEM((4, XL * YL, ZL), f32),
                col, col,
                pltpu.VMEM((4, XL * YL, ZL), f32),
                pltpu.VMEM((4 * XL, YL), f32),
                pltpu.VMEM((XL, YL), jnp.int32),
                pltpu.VMEM((4, 2, 4, YL, ZL), f32),
                pltpu.VMEM((4, 2, 4, XL, ZL), f32),
                pltpu.VMEM((4, 2, 4, XL, ZL), f32),
                pltpu.VMEM((2, 8, ZL), f32),
                pltpu.VMEM((2, N1, 8, ZL), f32),
                pltpu.VMEM((2, 8, ZL), f32),
                pltpu.VMEM((2, N2, 8, ZL), f32),
                col, col,
                dma((XL + 3,)), dma((4, 4)), dma((4, 4)),
                dma((2, N1)), dma((2, N1)), dma((2, N2)), dma((2, N2)),
                dma((NGC,)), dma((NGC,)),
            ],
            compiler_params=pltpu.CompilerParams(collective_id=0, has_side_effects=True),
        )(model.reshape(XL * YL, ZL), freq_sq, source.reshape(4, XL, YL, ZL),
          observed.reshape(4 * XL, YL), receiver_depth)
        return field.reshape(2, 2, XL, YL, ZL), grad.reshape(XL, YL, ZL)

    in_specs = (
        P("gx", "gy", None),
        P("af"),
        P("af", None, "gx", "gy", None),
        P("af", None, "gx", "gy"),
        P("gx", "gy"),
    )
    out_specs = (P("af", None, "gx", "gy", None), P("gx", "gy", None))
    return jax.shard_map(
        on_device, mesh=mesh, in_specs=in_specs, out_specs=out_specs, check_vma=False
    )
```

time: 1230 us -> 61.8 us (0.05)
  blocking collectives: 882 us -> 0 us
  waiting for transfers between devices: 210 us -> 0 us
  starting transfers between devices: 67.7 us -> 0 us
  Pallas kernels: 0 us -> 57.1 us
  other arithmetic: 34.7 us -> 0 us
  local copies, waits for them, and re-layouts: 18.4 us -> 3.93 us
  between operations: 14.6 us -> 0.65 us
    psum x3 -> x0, blocking collectives: 882 us -> none  [the longest x2 592 us: squares(): return lax.psum(inner(values, values), ('gx', 'gy'))]
    psum x1 -> x0, waiting for transfers between devices: 200 us -> none  [on_device(): gradient = lax.psum(local_terms, 'af')]
    ppermute x24 -> x0, starting transfers between devices: 67.7 us -> none  [the longest x12 52.2 us: padded_2(): lax.ppermute(tail, axis, [(i, (i + 1) % count) for i in range(ends)])]
    pallas_call x0 -> x1, Pallas kernels: none -> 57.1 us  [on_device(): pl.pallas_call(functools.partial(kernel, (GX, GY, XL, YL, NGC)), out_shap...]
  transfers between devices with their start and end apart: 25 -> 0, of which waited for: 12 -> 0; matrix products, arithmetic and copies ran while one was open for 1% -> 0% of each run, Pallas kernels for 0% -> 0%
where the time goes in v1:
time: 61.8 us; the launch traced here: 61.7 us
  Pallas kernels  57.1 us (92%)
  local copies, waits for them, and re-layouts  3.93 us (6%)
  between operations  0.65 us (1%)
    pallas_call x1, Pallas kernels, on_device(): pl.pallas_call(functools.partial(kernel, (GX, GY, XL, YL, NGC)), out_shap...  57.1 us
    unnamed x4, local copies, waits for them, and re-layouts  3.93 us

profile of v1, /device:TPU:1, one launch (start us, length us, event | category | flops | bytes accessed | tf_op | source)
XLA Modules:
  0.0 61.7 jit_solution(9936197925728336674)
XLA Ops:
  0.6 57.1 %shard_map.68 = (f32[4096,128]{1,0:T(8,128)}, f32[1024,128]{1,0:T(8,128)}) custom-call(f32[1024,128]{1,0:T(8,128)} %bitcast.8, f32[2]{0:T(128)} %fsq.1, f32[4,32,32,128]{3,2,1,0:T(8,128)} %bitcast.5, f32[128,32]{1,0:T(8,128)} %bitcast.9, s32[32,32]{1,0:T(8,128)} %depth_h.1), custom_call_target="tpu_custom_call" | custom-call | tf_op jit(solution)/shard_map/pallas_call | solution.py:408
  57.7 0.0 copy-start
  57.7 3.1 %copy.9 = f32[2,2,32,32,128]{4,3,2,1,0:T(8,128)} copy(f32[2,2,32,32,128]{4,3,2,1,0:T(8,128)} %bitcast.6) | data formatting | bytes 4194304
  60.9 0.0 copy-done
  60.9 0.8 %copy.10 = f32[32,32,128]{2,1,0:T(8,128)} copy(f32[32,32,128]{2,1,0:T(8,128)S(1)} %bitcast.7) | data formatting | bytes 1048576
Async XLA Ops:
  57.7 3.1 %copy-start = (f32[1024,128]{1,0:T(8,128)S(1)}, f32[1024,128]{1,0:T(8,128)}, u32[]{:S(2)}) copy-start(f32[1024,128]{1,0:T(8,128)} %get-tuple-element.5) | copy-start | bytes 1572868

commit v2 on v1

v2 whole, which is shorter than its diff:
```python
import functools

import jax
import jax.numpy as jnp
from jax import lax
from jax.experimental import pallas as pl
from jax.experimental.pallas import tpu as pltpu
from jax.sharding import PartitionSpec as P

MESH = pl.DeviceIdType.MESH
ATTENUATION = 0.2
PENALTY = 4.0


def kernel(dims, model_h, fsq, src_h, obs_h, depth_h, field_o, grad_o,
           S, B, U, Q, PP, M, W, WO, OB, DP, HX, HY, YS, A1R, A2R, GS, GR,
           load_sem, hs_sem, hr_sem, a1s_sem, a1r_sem, a2s_sem, a2r_sem, tok_sem, gs_sem, gr_sem):
    GX, GY, XL, YL, NGC = dims
    PX = XL + 2
    NT = YL // 8
    XT = XL // 8
    N1 = GX * 2
    N2 = GY // 2
    gx = lax.axis_index("gx")
    gy = lax.axis_index("gy")
    af = lax.axis_index("af")

    def first(j):
        r = lax.rem(gx * 2 + lax.rem(gy, 2) + j, N1)
        return r // 2, (gy // 2) * 2 + lax.rem(r, 2)

    def second(j):
        return lax.rem(gy // 2 + j, N2) * 2 + lax.rem(gy, 2)

    def axis_peer(n, sign, axis):
        at, size, name = ((gx, GX, "gx"), (gy, GY, "gy"))[axis]
        return (at >= n, {name: at - n}) if sign < 0 else (at < size - n, {name: at + n})

    barrier = pltpu.get_barrier_semaphore()
    pl.semaphore_signal(barrier, inc=1, device_id={"af": 1 - af}, device_id_type=MESH)
    peers = jnp.int32(1)
    for axis in range(2):
        for sign in (-1, 1):
            cond, dev = axis_peer(1, sign, axis)
            peers = peers + cond.astype(jnp.int32)

            @pl.when(cond)
            def _():
                pl.semaphore_signal(barrier, inc=1, device_id=dev, device_id_type=MESH)

    def tell(r, n):
        for axis in range(2):
            for sign in (-1, 1):
                cond, dev = axis_peer(n, sign, axis)

                @pl.when(cond)
                def _():
                    pl.semaphore_signal(tok_sem.at[r, 2 * axis + (sign < 0)], inc=1, device_id=dev,
                                        device_id_type=MESH)

    def told(r, n):
        for axis in range(2):
            for sign in (-1, 1):
                cond, dev = axis_peer(n, sign, axis)

                @pl.when(cond)
                def _():
                    pl.semaphore_wait(tok_sem.at[r, 2 * axis + (sign > 0)], 1)

    loads = [
        pltpu.make_async_copy(depth_h, DP, load_sem.at[4]),
        pltpu.make_async_copy(obs_h, OB, load_sem.at[5]),
        pltpu.make_async_copy(model_h, M, load_sem.at[6]),
    ] + [
        pltpu.make_async_copy(src_h.at[c], S.at[c, pl.ds(YL, XL * YL), :], load_sem.at[c]) for c in range(4)
    ]
    for cp in loads:
        cp.start()

    zero = jnp.zeros((8, 128), jnp.float32)

    for ref in (S, B, U, Q):
        for c in range(4):
            for xx in (0, PX - 1):
                for t in range(NT):
                    ref[c, pl.ds(xx * YL + t * 8, 8), :] = zero

    def clear_halo(ref, side, count):
        for e in range(4):
            for c in range(4):
                for r in range(0, count, 8):
                    ref[e, side, c, pl.ds(r, 8), :] = zero

    for cond, ref, side, count in ((gx == 0, HX, 0, YL), (gx == GX - 1, HX, 1, YL),
                                   (gy == 0, HY, 0, XL), (gy == GY - 1, HY, 1, XL)):
        pl.when(cond)(functools.partial(clear_halo, ref, side, count))

    def copies(e, V):
        out = []
        plan = (
            (gy > 0, {"gy": gy - 1}, YS.at[e, 0], HY.at[e, 1], 2, 3),
            (gy < GY - 1, {"gy": gy + 1}, YS.at[e, 1], HY.at[e, 0], 3, 2),
            (gx > 0, {"gx": gx - 1}, V.at[:, pl.ds(YL, YL), :],
             HX.at[e, 1], 0, 1),
            (gx < GX - 1, {"gx": gx + 1}, V.at[:, pl.ds(XL * YL, YL), :],
             HX.at[e, 0], 1, 0),
        )
        for cond, dev, s, d, mine, theirs in plan:
            out.append((cond, pltpu.make_async_remote_copy(
                src_ref=s, dst_ref=d, send_sem=hs_sem.at[e, mine], recv_sem=hr_sem.at[e, theirs],
                device_id=dev, device_id_type=MESH)))
        return out

    def send(e, V):
        for side, yy in ((0, 0), (1, YL - 1)):
            for c in range(4):
                for k in range(XT):
                    YS[e, side, c, pl.ds(k * 8, 8), :] = V[c, pl.ds((1 + 8 * k) * YL + yy, 8, stride=YL), :]
        for cond, cp in copies(e, V):
            pl.when(cond)(cp.start)

    def arrive(e, V):
        cps = copies(e, V)
        for (cond, _), (_, cp) in zip(cps, (cps[1], cps[0], cps[3], cps[2])):
            pl.when(cond)(cp.wait_recv)

    def drain(e, V):
        for cond, cp in copies(e, V):
            pl.when(cond)(cp.wait_send)

    lane = lax.broadcasted_iota(jnp.int32, (8, 128), 1)
    at_first = lane == 0
    at_last = lane == 127
    sq = [fsq[0], fsq[1]]

    sub = lax.broadcasted_iota(jnp.int32, (8, 128), 0)
    UN = 2

    def around(V, c, o, t):
        cen = V[c, pl.ds(o, 8), :]
        total = V[c, pl.ds(o - YL, 8), :] + V[c, pl.ds(o + YL, 8), :]
        ym, yp = V[c, pl.ds(o - 1, 8), :], V[c, pl.ds(o + 1, 8), :]
        if t == 0:
            ym = jnp.where(sub == 0, 0.0, ym)
        if t == NT - 1:
            yp = jnp.where(sub == 7, 0.0, yp)
        total = total + (ym + yp)
        lo = jnp.where(at_first, 0.0, pltpu.roll(cen, 1, 1))
        hi = jnp.where(at_last, 0.0, pltpu.roll(cen, 127, 1))
        return cen, total + (lo + hi)

    def sweep(V, sign, finish, carry):
        def body(i, carry):
            for p in range(UN):
                r0 = pl.multiple_of(i * (UN * YL), 8) + p * YL
                for t in range(NT):
                    m = M[pl.ds(r0 + t * 8, 8), :]
                    for f in range(2):
                        k = sq[f] * m
                        cr = 6.0 - k
                        ci = (sign * ATTENUATION) * k
                        o = r0 + YL + t * 8
                        re, nre = around(V, 2 * f, o, t)
                        im, nim = around(V, 2 * f + 1, o, t)
                        out = (cr * re - ci * im - nre, cr * im + ci * re - nim)
                        carry = finish(f, o, r0 + t * 8, (re, im), out, carry)
            return carry
        return lax.fori_loop(0, XL // UN, body, carry)

    def correct(e, rows, step, carry):
        for side in range(2):
            for c in range(4):
                for t in range(NT):
                    idx = rows(c, 1 + side * (XL - 1), t * 8, False)
                    carry = step(c // 2, idx, HX[e, side, c, pl.ds(t * 8, 8), :], carry)
        for side in range(2):
            for c in range(4):
                for k in range(XT):
                    idx = rows(c, 1 + 8 * k, side * (YL - 1), True)
                    carry = step(c // 2, idx, HY[e, side, c, pl.ds(k * 8, 8), :], carry)
        return carry

    def padded(c, xx, yy, strided):
        o = xx * YL + yy
        return c, pl.ds(o, 8, stride=YL) if strided else pl.ds(o, 8)

    def compact(c, xx, yy, strided):
        return padded(c, xx - 1, yy, strided)

    loads[0].wait()
    loads[1].wait()
    dt = jnp.transpose(jnp.concatenate(
        [DP[...].astype(jnp.float32), jnp.zeros((XL, 128 - YL), jnp.float32)], axis=1))
    ot = jnp.transpose(jnp.concatenate(
        [OB[...], jnp.zeros((4 * XL, 128 - YL), jnp.float32)], axis=1))
    lanef = lane.astype(jnp.float32)
    for x in range(XL):
        for t in range(NT):
            d = jnp.broadcast_to(dt[t * 8:t * 8 + 8, x:x + 1], (8, 128))
            w = jnp.where(lanef == d, PENALTY, 0.0)
            W[pl.ds(x * YL + t * 8, 8), :] = w
            for c in range(4):
                ob = jnp.broadcast_to(ot[t * 8:t * 8 + 8, c * XL + x:c * XL + x + 1], (8, 128))
                WO[c, pl.ds(x * YL + t * 8, 8), :] = w * ob

    for cp in loads[2:]:
        cp.wait()
    pl.semaphore_wait(barrier, peers)
    send(0, S)

    def finish_b(f, o, r, cen, out, carry):
        acc = carry[f]
        for c in range(2):
            v = out[c] + WO[2 * f + c, pl.ds(r, 8), :]
            B[2 * f + c, pl.ds(o, 8), :] = v
            acc = acc + v * v
        return tuple(acc if i == f else carry[i] for i in range(2))

    def fix_field(ref):
        def step(f, idx, h, carry):
            old = ref[idx[0], idx[1], :]
            new = old - h
            ref[idx[0], idx[1], :] = new
            d = h * (h - 2.0 * old)
            return tuple(carry[i] + d if i == f else carry[i] for i in range(2))
        return step

    rr = sweep(S, -1.0, finish_b, (zero, zero))
    arrive(0, S)
    rr = correct(0, padded, fix_field(B), rr)
    send(1, B)
    tell(0, 2)

    def finish_u(f, o, r, cen, out, carry):
        acc = carry[f]
        for c in range(2):
            U[2 * f + c, pl.ds(o, 8), :] = out[c]
            acc = acc + out[c] * out[c]
        return tuple(acc if i == f else carry[i] for i in range(2))

    dq = sweep(B, 1.0, finish_u, (zero, zero))
    arrive(1, B)
    dq = correct(1, padded, fix_field(U), dq)
    send(2, U)
    told(0, 2)
    tell(1, 4)

    def finish_q(f, o, r, cen, out, carry):
        dq, qq = carry[f], carry[2 + f]
        w = W[pl.ds(r, 8), :]
        for c in range(2):
            b = B[2 * f + c, pl.ds(o, 8), :]
            wb = w * b
            v = out[c] + wb
            Q[2 * f + c, pl.ds(o, 8), :] = v
            dq = dq + wb * b
            qq = qq + v * v
        carry = list(carry)
        carry[f], carry[2 + f] = dq, qq
        return tuple(carry)

    carry = sweep(U, -1.0, finish_q, tuple(dq) + (zero, zero))
    dq, qq = carry[:2], carry[2:]
    arrive(2, U)
    qq = correct(2, padded, fix_field(Q), qq)
    send(3, Q)
    told(1, 4)
    tell(2, 8)

    def finish_p(f, o, r, cen, out, carry):
        acc = carry[f]
        w = W[pl.ds(r, 8), :]
        for c in range(2):
            PP[2 * f + c, pl.ds(r, 8), :] = out[c]
            acc = acc + (out[c] * out[c] + w * (cen[c] * cen[c]))
        return tuple(acc if i == f else carry[i] for i in range(2))

    qmq = sweep(Q, 1.0, finish_p, (zero, zero))
    arrive(3, Q)
    qmq = correct(3, compact, fix_field(PP), qmq)
    told(2, 8)

    group = lane // 16

    def first_copy(j, slot):
        px, py = first(j)
        return pltpu.make_async_remote_copy(
            src_ref=A1R.at[pl.ds(0, 1), :], dst_ref=A1R.at[pl.ds(slot, 1), :],
            send_sem=a1s_sem.at[j], recv_sem=a1r_sem.at[slot],
            device_id={"gx": px, "gy": py}, device_id_type=MESH)

    def second_copy(j, slot):
        return pltpu.make_async_remote_copy(
            src_ref=A2R.at[pl.ds(0, 1), :], dst_ref=A2R.at[pl.ds(slot, 1), :],
            send_sem=a2s_sem.at[j], recv_sem=a2r_sem.at[slot],
            device_id={"gy": second(j)}, device_id_type=MESH)

    def reduce_first(parts):
        mix = zero
        for i, v in enumerate(parts):
            for shift in (64, 32, 16):
                v = v + pltpu.roll(v, shift, 1)
            mix = jnp.where(group == i, v, mix)
        A1R[pl.ds(0, 1), :] = jnp.sum(mix, axis=0, keepdims=True)
        for j in range(1, N1):
            first_copy(j, N1 - j).start()

    def reduce_second():
        for j in range(1, N1):
            first_copy(j, j).wait_recv()
        A2R[pl.ds(0, 1), :] = jnp.sum(A1R[...], axis=0, keepdims=True)
        for j in range(1, N2):
            second_copy(j, N2 - j).start()

    def reduce_end():
        for j in range(1, N2):
            second_copy(j, j).wait_recv()
        v = jnp.broadcast_to(jnp.sum(A2R[...], axis=0, keepdims=True), (8, 128))
        for shift in (8, 4, 2, 1):
            v = v + pltpu.roll(v, 128 - shift, 1)
        return v

    def reduce_drain():
        for j in range(1, N1):
            first_copy(j, j).wait_send()
        for j in range(1, N2):
            second_copy(j, j).wait_send()

    def row(sums, i):
        return jnp.broadcast_to(sums[:, 16 * i:16 * i + 1], (8, 128))

    reduce_first((rr[0], rr[1], dq[0], dq[1], qq[0], qq[1], qmq[0], qmq[1]))
    for e, V in enumerate((S, B, U, Q)):
        drain(e, V)
    reduce_second()
    sums = reduce_end()

    cb, cq = [], []
    for f in range(2):
        norm0, curv0, qq0, qmq0 = (row(sums, 2 * i + f) for i in range(4))
        alpha0 = norm0 / curv0
        norm1 = norm0 - alpha0 * (2.0 * curv0 - alpha0 * qq0)
        beta = norm1 / norm0
        rq = curv0 - alpha0 * qq0
        rmr = curv0 - alpha0 * (2.0 * qq0 - alpha0 * qmq0)
        alpha1 = norm1 / (rmr + beta * (2.0 * rq + beta * curv0))
        cb.append(alpha0 + alpha1 * (1.0 + beta))
        cq.append(-(alpha0 * alpha1))

    GROWS = XL * YL // NGC
    def grad_copy(g):
        return pltpu.make_async_remote_copy(
            src_ref=GS.at[pl.ds(g * GROWS, GROWS), :], dst_ref=GR.at[pl.ds(g * GROWS, GROWS), :],
            send_sem=gs_sem.at[g], recv_sem=gr_sem.at[g], device_id={"af": 1 - af}, device_id_type=MESH)

    def outputs(i, _):
        for p in range(UN):
            r0 = pl.multiple_of(i * (UN * YL), 8) + p * YL
            for t in range(NT):
                r = r0 + t * 8
                g = zero
                for f in range(2):
                    fld, mis = [], []
                    for c in range(2):
                        n = 2 * f + c
                        v = cb[f] * B[n, pl.ds(r + YL, 8), :] + cq[f] * Q[n, pl.ds(r + YL, 8), :]
                        field_o[n, pl.ds(r, 8), :] = v
                        fld.append(v)
                        mis.append(cb[f] * U[n, pl.ds(r + YL, 8), :] + cq[f] * PP[n, pl.ds(r, 8), :]
                                   - S[n, pl.ds(r + YL, 8), :])
                    wr = -fld[0] - ATTENUATION * fld[1]
                    wi = ATTENUATION * fld[0] - fld[1]
                    g = g + sq[f] * (wr * mis[0] + wi * mis[1])
                GS[pl.ds(r, 8), :] = g
        return 0

    for g in range(NGC):
        lax.fori_loop(g * (XL // NGC // UN), (g + 1) * (XL // NGC // UN), outputs, 0)
        grad_copy(g).start()

    for g in range(NGC):
        grad_copy(g).wait_recv()

        def add(i, _):
            for n in range(8):
                o = pl.multiple_of(i * 64, 8) + n * 8
                grad_o[pl.ds(o, 8), :] = GS[pl.ds(o, 8), :] + GR[pl.ds(o, 8), :]
            return 0

        lax.fori_loop(g * GROWS // 64, (g + 1) * GROWS // 64, add, 0)

    for g in range(NGC):
        grad_copy(g).wait_send()
    reduce_drain()


def solution(mesh):
    GX, GY = mesh.shape["gx"], mesh.shape["gy"]

    def on_device(model, freq_sq, source, observed, receiver_depth):
        XL, YL, ZL = model.shape
        PX = XL + 2
        f32 = jnp.float32
        N1, N2 = GX * 2, GY // 2
        NGC = 4
        big = pltpu.VMEM((4, PX * YL, ZL), f32)
        col = pltpu.VMEM((XL * YL, ZL), f32)
        dma = pltpu.SemaphoreType.DMA
        field, grad = pl.pallas_call(
            functools.partial(kernel, (GX, GY, XL, YL, NGC)),
            out_shape=(jax.ShapeDtypeStruct((4, XL * YL, ZL), f32),
                       jax.ShapeDtypeStruct((XL * YL, ZL), f32)),
            in_specs=[pl.BlockSpec(memory_space=pltpu.HBM),
                      pl.BlockSpec(memory_space=pltpu.SMEM),
                      pl.BlockSpec(memory_space=pltpu.HBM),
                      pl.BlockSpec(memory_space=pltpu.HBM),
                      pl.BlockSpec(memory_space=pltpu.HBM)],
            out_specs=(pl.BlockSpec(memory_space=pltpu.VMEM),) * 2,
            scratch_shapes=[
                big, big, big, big,
                pltpu.VMEM((4, XL * YL, ZL), f32),
                col, col,
                pltpu.VMEM((4, XL * YL, ZL), f32),
                pltpu.VMEM((4 * XL, YL), f32),
                pltpu.VMEM((XL, YL), jnp.int32),
                pltpu.VMEM((4, 2, 4, YL, ZL), f32),
                pltpu.VMEM((4, 2, 4, XL, ZL), f32),
                pltpu.VMEM((4, 2, 4, XL, ZL), f32),
                pltpu.VMEM((N1, ZL), f32),
                pltpu.VMEM((N2, ZL), f32),
                col, col,
                dma((7,)), dma((4, 4)), dma((4, 4)),
                dma((N1,)), dma((N1,)), dma((N2,)), dma((N2,)),
                pltpu.SemaphoreType.REGULAR((3, 4)),
                dma((NGC,)), dma((NGC,)),
            ],
            compiler_params=pltpu.CompilerParams(
                collective_id=0, has_side_effects=True, vmem_limit_bytes=26 * 2**20),
        )(*[pltpu.with_memory_space_constraint(a, pltpu.HBM) for a in (
            model.reshape(XL * YL, ZL), freq_sq, source.reshape(4, XL * YL, ZL),
            observed.reshape(4 * XL, YL), receiver_depth)])
        return field.reshape(2, 2, XL, YL, ZL), grad.reshape(XL, YL, ZL)

    in_specs = (
        P("gx", "gy", None),
        P("af"),
        P("af", None, "gx", "gy", None),
        P("af", None, "gx", "gy"),
        P("gx", "gy"),
    )
    out_specs = (P("af", None, "gx", "gy", None), P("gx", "gy", None))
    return jax.shard_map(
        on_device, mesh=mesh, in_specs=in_specs, out_specs=out_specs, check_vma=False
    )
```

time: 61.8 us -> 56 us (0.906)
  Pallas kernels: 57.1 us -> 53.1 us
  local copies, waits for them, and re-layouts: 3.93 us -> 2.11 us
    pallas_call x1, Pallas kernels: 57.1 us -> 53.1 us  [on_device(): pl.pallas_call(functools.partial(kernel, (GX, GY, XL, YL, NGC)), out_shap...]
    unnamed x4 -> x2, local copies, waits for them, and re-layouts: 3.93 us -> 2.11 us
where the time goes in v2:
time: 56 us; the launch traced here: 55.8 us
  Pallas kernels  53.1 us (95%)
  local copies, waits for them, and re-layouts  2.11 us (4%)
  between operations  0.64 us (1%)
    pallas_call x1, Pallas kernels, on_device(): pl.pallas_call(functools.partial(kernel, (GX, GY, XL, YL, NGC)), out_shap...  53.1 us
    unnamed x2, local copies, waits for them, and re-layouts  2.11 us

profile of v2, /device:TPU:1, one launch (start us, length us, event | category | flops | bytes accessed | tf_op | source)
XLA Modules:
  0.0 55.8 jit_solution(8210770866804356122)
XLA Ops:
  0.6 53.1 %shard_map.68 = (f32[4,1024,128]{2,1,0:T(8,128)S(1)}, f32[1024,128]{1,0:T(8,128)S(1)}) custom-call(f32[1024,128]{1,0:T(8,128)} %bitcast.8, f32[2]{0:T(128)} %fsq.1, f32[4,1024,128]{2,1,0:T(8,128)} %bitcast.7, f32[128,32]{1,0:T(8,128)} %bitcast.9, s32[32,32]{1,0:T(8,128)} %depth_h.1), custom_call_target="tpu_custom_call" | custom-call | tf_op jit(solution)/shard_map/pallas_call | solution.py:409
  53.7 1.3 %copy.9 = f32[2,2,32,32,128]{4,3,2,1,0:T(8,128)} copy(f32[2,2,32,32,128]{4,3,2,1,0:T(8,128)S(1)} %bitcast.5) | data formatting | bytes 4194304
  55.0 0.8 %copy.10 = f32[32,32,128]{2,1,0:T(8,128)} copy(f32[32,32,128]{2,1,0:T(8,128)S(1)} %bitcast.6) | data formatting | bytes 1048576

commit v3 on v2

--- a/solution.py
+++ b/solution.py
@@ -13,8 +13,10 @@
 
 
 def kernel(dims, model_h, fsq, src_h, obs_h, depth_h, field_o, grad_o,
-           S, B, U, Q, PP, M, W, WO, OB, DP, HX, HY, YS, A1R, A2R, GS, GR,
-           load_sem, hs_sem, hr_sem, a1s_sem, a1r_sem, a2s_sem, a2r_sem, tok_sem, gs_sem, gr_sem):
+           S, B, U, Q, PP, M, W, WO, OB, DP, X1, X2, Y1, Y2, YS, MX, MY, MYS, IS, IR, CS, CR, WH, WOH, BH,
+           A1R, A2R, GS, GR,
+           load_sem, hs_sem, hr_sem, ms_sem, mr_sem, cs_sem, cr_sem,
+           a1s_sem, a1r_sem, a2s_sem, a2r_sem, tok_sem, gs_sem, gr_sem):
     GX, GY, XL, YL, NGC = dims
     PX = XL + 2
     NT = YL // 8
@@ -85,48 +87,113 @@
                 for t in range(NT):
                     ref[c, pl.ds(xx * YL + t * 8, 8), :] = zero
 
-    def clear_halo(ref, side, count):
-        for e in range(4):
+    def clear(ref, side, count):
+        for e in range(2):
             for c in range(4):
                 for r in range(0, count, 8):
-                    ref[e, side, c, pl.ds(r, 8), :] = zero
-
-    for cond, ref, side, count in ((gx == 0, HX, 0, YL), (gx == GX - 1, HX, 1, YL),
-                                   (gy == 0, HY, 0, XL), (gy == GY - 1, HY, 1, XL)):
-        pl.when(cond)(functools.partial(clear_halo, ref, side, count))
-
-    def copies(e, V):
-        out = []
-        plan = (
-            (gy > 0, {"gy": gy - 1}, YS.at[e, 0], HY.at[e, 1], 2, 3),
-            (gy < GY - 1, {"gy": gy + 1}, YS.at[e, 1], HY.at[e, 0], 3, 2),
-            (gx > 0, {"gx": gx - 1}, V.at[:, pl.ds(YL, YL), :],
-             HX.at[e, 1], 0, 1),
-            (gx < GX - 1, {"gx": gx + 1}, V.at[:, pl.ds(XL * YL, YL), :],
-             HX.at[e, 0], 1, 0),
-        )
-        for cond, dev, s, d, mine, theirs in plan:
-            out.append((cond, pltpu.make_async_remote_copy(
-                src_ref=s, dst_ref=d, send_sem=hs_sem.at[e, mine], recv_sem=hr_sem.at[e, theirs],
-                device_id=dev, device_id_type=MESH)))
-        return out
-
-    def send(e, V):
-        for side, yy in ((0, 0), (1, YL - 1)):
+                    ref[e, side, c, pl.ds(8 + r, 8), :] = zero
+
+    has = ((gx > 0, gx < GX - 1), (gy > 0, gy < GY - 1))
+    for side in range(2):
+        pl.when(jnp.logical_not(has[0][side]))(functools.partial(clear, X1, side, YL))
+        pl.when(jnp.logical_not(has[1][side]))(functools.partial(clear, Y1, side, XL))
+    for sx in range(2):
+        for sy in range(2):
+            @pl.when(jnp.logical_not(jnp.logical_and(has[0][sx], has[1][sy])))
+            def _():
+                for e in range(2):
+                    CR[e, 2 * sx + sy] = zero
+
+    for face in range(4):
+        @pl.when(jnp.logical_not(has[face // 2][face % 2]))
+        def _():
+            IR[face] = zero
+
+    def remote(src, dst, ssem, rsem, dev):
+        return pltpu.make_async_remote_copy(
+            src_ref=src, dst_ref=dst, send_sem=ssem, recv_sem=rsem, device_id=dev, device_id_type=MESH)
+
+    def face_dev(face):
+        axis, side = face // 2, face % 2
+        step = 2 * side - 1
+        return has[axis][side], ({"gx": gx + step} if axis == 0 else {"gy": gy + step})
+
+    def layer_copy(e, l, V, face):
+        axis, side = face // 2, face % 2
+        there = 1 - side
+        if axis == 0:
+            plane = l if side == 0 else XL - 1 - l
+            src = V.at[:, pl.ds((1 + plane) * YL, YL), :]
+            dst = X1.at[e, there, :, pl.ds(8, YL), :] if l == 0 else X2.at[e, there]
+        else:
+            src = YS.at[e, side, l]
+            dst = Y1.at[e, there, :, pl.ds(8, XL), :] if l == 0 else Y2.at[e, there]
+        cond, dev = face_dev(face)
+        return cond, remote(src, dst, hs_sem.at[e, l, face], hr_sem.at[e, l, 2 * axis + there], dev)
+
+    def model_copy(face):
+        axis, side = face // 2, face % 2
+        there = 1 - side
+        if axis == 0:
+            src, dst = M.at[pl.ds(side * (XL - 1) * YL, YL), :], MX.at[there]
+        else:
+            src, dst = MYS.at[side], MY.at[there]
+        cond, dev = face_dev(face)
+        return cond, remote(src, dst, ms_sem.at[0, face], mr_sem.at[0, 2 * axis + there], dev)
+
+    def info_copy(face):
+        axis, side = face // 2, face % 2
+        there = 2 * axis + 1 - side
+        cond, dev = face_dev(face)
+        return cond, remote(IS.at[face], IR.at[there], ms_sem.at[1, face], mr_sem.at[1, there], dev)
+
+    def corner_copy(e, k):
+        sx, sy = k // 2, k % 2
+        return jnp.logical_and(has[0][sx], has[1][sy]), remote(
+            CS.at[e, k, pl.ds(0, 4), :], CR.at[e, 3 - k, pl.ds(0, 4), :], cs_sem.at[e, k], cr_sem.at[e, 3 - k],
+            {"gx": gx + (2 * sx - 1), "gy": gy + (2 * sy - 1)})
+
+    FACES = (2, 3, 0, 1)
+    other = lambda face: face ^ 1
+
+    def start_all(copies):
+        for cond, cp in copies:
+            pl.when(cond)(cp.start)
+
+    def drain_all(copies):
+        for cond, cp in copies:
+            pl.when(cond)(cp.wait_send)
+
+    def arrive_all(make, faces):
+        for face in faces:
+            cond, _ = face_dev(face)
+            pl.when(cond)(make(other(face))[1].wait_recv)
+
+    def arrive_layer(e, l, V):
+        arrive_all(lambda face: layer_copy(e, l, V, face), FACES)
+
+    def arrive_corners(e):
+        for k in range(4):
+            pl.when(jnp.logical_and(has[0][k // 2], has[1][k % 2]))(corner_copy(e, 3 - k)[1].wait_recv)
+        for k in range(4):
+            sx, sy = k // 2, k % 2
+            for c in range(4):
+                v = CR[e, k, pl.ds(c, 1), :]
+                X1[e, sx, c, pl.ds(8 + YL if sy else 7, 1), :] = v
+                Y1[e, sy, c, pl.ds(8 + XL if sx else 7, 1), :] = v
+
+    def pack_layer(e, l, V):
+        for side in range(2):
+            y = l if side == 0 else YL - 1 - l
             for c in range(4):
                 for k in range(XT):
-                    YS[e, side, c, pl.ds(k * 8, 8), :] = V[c, pl.ds((1 + 8 * k) * YL + yy, 8, stride=YL), :]
-        for cond, cp in copies(e, V):
-            pl.when(cond)(cp.start)
-
-    def arrive(e, V):
-        cps = copies(e, V)
-        for (cond, _), (_, cp) in zip(cps, (cps[1], cps[0], cps[3], cps[2])):
-            pl.when(cond)(cp.wait_recv)
-
-    def drain(e, V):
-        for cond, cp in copies(e, V):
-            pl.when(cond)(cp.wait_send)
+                    YS[e, side, l, c, pl.ds(k * 8, 8), :] = V[c, pl.ds((1 + 8 * k) * YL + y, 8, stride=YL), :]
+
+    def pack_corners(e, V):
+        for k in range(4):
+            o = (1 + (XL - 1) * (k // 2)) * YL + (YL - 1) * (k % 2)
+            for c in range(4):
+                CS[e, k, pl.ds(c, 1), :] = V[c, pl.ds(o, 1), :]
 
     lane = lax.broadcasted_iota(jnp.int32, (8, 128), 1)
     at_first = lane == 0
@@ -149,35 +216,90 @@
         hi = jnp.where(at_last, 0.0, pltpu.roll(cen, 127, 1))
         return cen, total + (lo + hi)
 
+    def coefs(f, m, sign):
+        k = sq[f] * m
+        return 6.0 - k, (sign * ATTENUATION) * k
+
+    def tiles_of(V, sign, finish, r0, tiles, carry):
+        for t in tiles:
+            m = M[pl.ds(r0 + t * 8, 8), :]
+            for f in range(2):
+                cr, ci = coefs(f, m, sign)
+                o = r0 + YL + t * 8
+                re, nre = around(V, 2 * f, o, t)
+                im, nim = around(V, 2 * f + 1, o, t)
+                out = (cr * re - ci * im - nre, cr * im + ci * re - nim)
+                carry = finish(f, o, r0 + t * 8, (re, im), out, carry)
+        return carry
+
+    def planes(V, sign, finish, carry, lo, hi, un, tiles):
+        def body(i, carry):
+            for p in range(un):
+                r0 = pl.multiple_of(i * (un * YL), 8) + (lo + p) * YL
+                carry = tiles_of(V, sign, finish, r0, tiles, carry)
+            return carry
+        if not tiles:
+            return carry
+        return lax.fori_loop(0, (hi - lo) // un, body, carry)
+
     def sweep(V, sign, finish, carry):
-        def body(i, carry):
-            for p in range(UN):
-                r0 = pl.multiple_of(i * (UN * YL), 8) + p * YL
-                for t in range(NT):
-                    m = M[pl.ds(r0 + t * 8, 8), :]
-                    for f in range(2):
-                        k = sq[f] * m
-                        cr = 6.0 - k
-                        ci = (sign * ATTENUATION) * k
-                        o = r0 + YL + t * 8
-                        re, nre = around(V, 2 * f, o, t)
-                        im, nim = around(V, 2 * f + 1, o, t)
-                        out = (cr * re - ci * im - nre, cr * im + ci * re - nim)
-                        carry = finish(f, o, r0 + t * 8, (re, im), out, carry)
+        return planes(V, sign, finish, carry, 0, XL, UN, range(NT))
+
+    def sweep_inner(V, sign, finish, carry):
+        return planes(V, sign, finish, carry, 2, XL - 2, 4, range(1, NT - 1))
+
+    def sweep_outer(V, sign, finish, carry):
+        carry = planes(V, sign, finish, carry, 2, XL - 2, 4, (0, NT - 1))
+        def ends(i, carry):
+            for p in range(2):
+                r0 = pl.multiple_of(i * ((XL - 2) * YL), 8) + p * YL
+                carry = tiles_of(V, sign, finish, r0, range(NT), carry)
             return carry
-        return lax.fori_loop(0, XL // UN, body, carry)
-
-    def correct(e, rows, step, carry):
-        for side in range(2):
+        return lax.fori_loop(0, 2, ends, carry)
+
+    def strip(e, V, face, finish, carry):
+        axis, side = face // 2, face % 2
+        H1, H2, MH, L = (X1, X2, MX, YL) if axis == 0 else (Y1, Y2, MY, XL)
+        for k in range(L // 8):
+            m = MH[side, pl.ds(8 * k, 8), :]
+            for f in range(2):
+                cr, ci = coefs(f, m, -1.0)
+                cen, nb = [], []
+                for c in (2 * f, 2 * f + 1):
+                    v = H1[e, side, c, pl.ds(8 + 8 * k, 8), :]
+                    if axis == 0:
+                        inward = V[c, pl.ds((1 + side * (XL - 1)) * YL + 8 * k, 8), :]
+                    else:
+                        inward = V[c, pl.ds((1 + 8 * k) * YL + side * (YL - 1), 8, stride=YL), :]
+                    total = (H2[e, side, c, pl.ds(8 * k, 8), :] + inward) + (
+                        H1[e, side, c, pl.ds(7 + 8 * k, 8), :] + H1[e, side, c, pl.ds(9 + 8 * k, 8), :])
+                    lo = jnp.where(at_first, 0.0, pltpu.roll(v, 1, 1))
+                    hi = jnp.where(at_last, 0.0, pltpu.roll(v, 127, 1))
+                    cen.append(v)
+                    nb.append(total + (lo + hi))
+                out = (cr * cen[0] - ci * cen[1] - nb[0], cr * cen[1] + ci * cen[0] - nb[1])
+                carry = finish(face, k, f, out, carry)
+        return carry
+
+    def on_face(rows, face, c, k):
+        axis, side = face // 2, face % 2
+        if axis == 0:
+            return rows(c, 1 + side * (XL - 1), 8 * k, False)
+        return rows(c, 1 + 8 * k, side * (YL - 1), True)
+
+    def take(ref, idx, h, f, carry):
+        old = ref[idx[0], idx[1], :]
+        ref[idx[0], idx[1], :] = old - h
+        d = h * (h - 2.0 * old)
+        return tuple(carry[i] + d if i == f else carry[i] for i in range(2))
+
+    def correct(e, ref, carry):
+        for face in range(4):
+            H1, L = (X1, YL) if face < 2 else (Y1, XL)
             for c in range(4):
-                for t in range(NT):
-                    idx = rows(c, 1 + side * (XL - 1), t * 8, False)
-                    carry = step(c // 2, idx, HX[e, side, c, pl.ds(t * 8, 8), :], carry)
-        for side in range(2):
-            for c in range(4):
-                for k in range(XT):
-                    idx = rows(c, 1 + 8 * k, side * (YL - 1), True)
-                    carry = step(c // 2, idx, HY[e, side, c, pl.ds(k * 8, 8), :], carry)
+                for k in range(L // 8):
+                    h = H1[e, face % 2, c, pl.ds(8 + 8 * k, 8), :]
+                    carry = take(ref, on_face(padded, face, c, k), h, c // 2, carry)
         return carry
 
     def padded(c, xx, yy, strided):
@@ -193,6 +315,30 @@
         [DP[...].astype(jnp.float32), jnp.zeros((XL, 128 - YL), jnp.float32)], axis=1))
     ot = jnp.transpose(jnp.concatenate(
         [OB[...], jnp.zeros((4 * XL, 128 - YL), jnp.float32)], axis=1))
+    for face in range(4):
+        IS[face] = zero
+    for side in range(2):
+        x, y = side * (XL - 1), side * (YL - 1)
+        for c in range(4):
+            IS[side, c:c + 1, 0:YL] = OB[c * XL + x:c * XL + x + 1, :]
+        IS[side, 4:5, 0:YL] = DP[x:x + 1, :].astype(jnp.float32)
+        IS[2 + side, 0:1, 0:4 * XL] = ot[y:y + 1, :]
+        IS[2 + side, 1:2, 0:XL] = dt[y:y + 1, :]
+    for cp in loads[2:]:
+        cp.wait()
+    for l in range(2):
+        pack_layer(0, l, S)
+    pack_corners(0, S)
+    for side in range(2):
+        for k in range(XT):
+            MYS[side, pl.ds(8 * k, 8), :] = M[pl.ds(8 * k * YL + side * (YL - 1), 8, stride=YL), :]
+    pl.semaphore_wait(barrier, peers)
+    start_all([layer_copy(0, 0, S, face) for face in FACES])
+    start_all([info_copy(face) for face in FACES])
+    start_all([layer_copy(0, 1, S, face) for face in FACES])
+    start_all([model_copy(face) for face in FACES])
+    tell(0, 1)
+
     lanef = lane.astype(jnp.float32)
     for x in range(XL):
         for t in range(NT):
@@ -203,11 +349,6 @@
                 ob = jnp.broadcast_to(ot[t * 8:t * 8 + 8, c * XL + x:c * XL + x + 1], (8, 128))
                 WO[c, pl.ds(x * YL + t * 8, 8), :] = w * ob
 
-    for cp in loads[2:]:
-        cp.wait()
-    pl.semaphore_wait(barrier, peers)
-    send(0, S)
-
     def finish_b(f, o, r, cen, out, carry):
         acc = carry[f]
         for c in range(2):
@@ -216,20 +357,10 @@
             acc = acc + v * v
         return tuple(acc if i == f else carry[i] for i in range(2))
 
-    def fix_field(ref):
-        def step(f, idx, h, carry):
-            old = ref[idx[0], idx[1], :]
-            new = old - h
-            ref[idx[0], idx[1], :] = new
-            d = h * (h - 2.0 * old)
-            return tuple(carry[i] + d if i == f else carry[i] for i in range(2))
-        return step
-
     rr = sweep(S, -1.0, finish_b, (zero, zero))
-    arrive(0, S)
-    rr = correct(0, padded, fix_field(B), rr)
-    send(1, B)
-    tell(0, 2)
+    told(0, 1)
+    start_all([corner_copy(0, k) for k in range(4)])
+    tell(1, 2)
 
     def finish_u(f, o, r, cen, out, carry):
         acc = carry[f]
@@ -238,12 +369,52 @@
             acc = acc + out[c] * out[c]
         return tuple(acc if i == f else carry[i] for i in range(2))
 
-    dq = sweep(B, 1.0, finish_u, (zero, zero))
-    arrive(1, B)
-    dq = correct(1, padded, fix_field(U), dq)
-    send(2, U)
-    told(0, 2)
-    tell(1, 4)
+    dq = sweep_inner(B, 1.0, finish_u, (zero, zero))
+    arrive_layer(0, 0, S)
+    rr = correct(0, B, rr)
+    told(1, 2)
+    tell(2, 4)
+    dq = sweep_outer(B, 1.0, finish_u, dq)
+
+    arrive_all(info_copy, FACES)
+    it = jnp.transpose(jnp.concatenate(
+        [IR[face] for face in range(4)] + [jnp.zeros((96, 128), jnp.float32)], axis=0))
+    for face in range(4):
+        L = YL if face < 2 else XL
+        for k in range(L // 8):
+            if face < 2:
+                d = it[8 * k:8 * k + 8, 8 * face + 4:8 * face + 5]
+                obs = [it[8 * k:8 * k + 8, 8 * face + c:8 * face + c + 1] for c in range(4)]
+            else:
+                d = it[8 * k:8 * k + 8, 8 * face + 1:8 * face + 2]
+                obs = [it[c * XL + 8 * k:c * XL + 8 * k + 8, 8 * face:8 * face + 1] for c in range(4)]
+            w = jnp.where(lanef == jnp.broadcast_to(d, (8, 128)), PENALTY, 0.0)
+            WH[face, pl.ds(8 * k, 8), :] = w
+            for c in range(4):
+                WOH[face, c, pl.ds(8 * k, 8), :] = w * jnp.broadcast_to(obs[c], (8, 128))
+
+    def finish_bh(face, k, f, out, carry):
+        cond, _ = face_dev(face)
+        for i in range(2):
+            c = 2 * f + i
+            v = jnp.where(cond, out[i] + WOH[face, c, pl.ds(8 * k, 8), :], 0.0)
+            BH[face, c, pl.ds(8 * k, 8), :] = v
+            carry = take(U, on_face(padded, face, c, k), v, f, carry)
+        return carry
+
+    arrive_all(model_copy, FACES)
+    arrive_layer(0, 1, S)
+    arrive_corners(0)
+    for face in FACES:
+        dq = strip(0, S, face, finish_bh, dq)
+    pack_corners(1, U)
+    for l in range(2):
+        pack_layer(1, l, U)
+    start_all([corner_copy(1, k) for k in range(4)])
+    for l in range(2):
+        start_all([layer_copy(1, l, U, face) for face in FACES])
+    told(2, 4)
+    tell(3, 8)
 
     def finish_q(f, o, r, cen, out, carry):
         dq, qq = carry[f], carry[2 + f]
@@ -261,12 +432,6 @@
 
     carry = sweep(U, -1.0, finish_q, tuple(dq) + (zero, zero))
     dq, qq = carry[:2], carry[2:]
-    arrive(2, U)
-    qq = correct(2, padded, fix_field(Q), qq)
-    send(3, Q)
-    told(1, 4)
-    tell(2, 8)
-
     def finish_p(f, o, r, cen, out, carry):
         acc = carry[f]
         w = W[pl.ds(r, 8), :]
@@ -275,10 +440,25 @@
             acc = acc + (out[c] * out[c] + w * (cen[c] * cen[c]))
         return tuple(acc if i == f else carry[i] for i in range(2))
 
-    qmq = sweep(Q, 1.0, finish_p, (zero, zero))
-    arrive(3, Q)
-    qmq = correct(3, compact, fix_field(PP), qmq)
-    told(2, 8)
+    qmq = sweep_inner(Q, 1.0, finish_p, (zero, zero))
+    arrive_layer(1, 0, U)
+    qq = correct(1, Q, qq)
+    told(3, 8)
+    qmq = sweep_outer(Q, 1.0, finish_p, qmq)
+
+    def finish_qh(face, k, f, out, carry):
+        cond, _ = face_dev(face)
+        w = WH[face, pl.ds(8 * k, 8), :]
+        for i in range(2):
+            c = 2 * f + i
+            v = jnp.where(cond, out[i] + w * BH[face, c, pl.ds(8 * k, 8), :], 0.0)
+            carry = take(PP, on_face(compact, face, c, k), v, f, carry)
+        return carry
+
+    arrive_layer(1, 1, U)
+    arrive_corners(1)
+    for face in FACES:
+        qmq = strip(1, U, face, finish_qh, qmq)
 
     group = lane // 16
 
@@ -330,8 +510,12 @@
         return jnp.broadcast_to(sums[:, 16 * i:16 * i + 1], (8, 128))
 
     reduce_first((rr[0], rr[1], dq[0], dq[1], qq[0], qq[1], qmq[0], qmq[1]))
-    for e, V in enumerate((S, B, U, Q)):
-        drain(e, V)
+    for e, V in ((0, S), (1, U)):
+        for l in range(2):
+            drain_all([layer_copy(e, l, V, face) for face in FACES])
+        drain_all([corner_copy(e, k) for k in range(4)])
+    drain_all([model_copy(face) for face in FACES])
+    drain_all([info_copy(face) for face in FACES])
     reduce_second()
     sums = reduce_end()
 
@@ -423,15 +607,27 @@
                 pltpu.VMEM((4, XL * YL, ZL), f32),
                 pltpu.VMEM((4 * XL, YL), f32),
                 pltpu.VMEM((XL, YL), jnp.int32),
-                pltpu.VMEM((4, 2, 4, YL, ZL), f32),
-                pltpu.VMEM((4, 2, 4, XL, ZL), f32),
-                pltpu.VMEM((4, 2, 4, XL, ZL), f32),
+                pltpu.VMEM((2, 2, 4, YL + 16, ZL), f32),
+                pltpu.VMEM((2, 2, 4, YL, ZL), f32),
+                pltpu.VMEM((2, 2, 4, XL + 16, ZL), f32),
+                pltpu.VMEM((2, 2, 4, XL, ZL), f32),
+                pltpu.VMEM((2, 2, 2, 4, XL, ZL), f32),
+                pltpu.VMEM((2, YL, ZL), f32),
+                pltpu.VMEM((2, XL, ZL), f32),
+                pltpu.VMEM((2, XL, ZL), f32),
+                pltpu.VMEM((4, 8, ZL), f32),
+                pltpu.VMEM((4, 8, ZL), f32),
+                pltpu.VMEM((2, 4, 8, ZL), f32),
+                pltpu.VMEM((2, 4, 8, ZL), f32),
+                pltpu.VMEM((4, max(XL, YL), ZL), f32),
+                pltpu.VMEM((4, 4, max(XL, YL), ZL), f32),
+                pltpu.VMEM((4, 4, max(XL, YL), ZL), f32),
                 pltpu.VMEM((N1, ZL), f32),
                 pltpu.VMEM((N2, ZL), f32),
                 col, col,
-                dma((7,)), dma((4, 4)), dma((4, 4)),
+                dma((7,)), dma((2, 2, 4)), dma((2, 2, 4)), dma((2, 4)), dma((2, 4)), dma((2, 4)), dma((2, 4)),
                 dma((N1,)), dma((N1,)), dma((N2,)), dma((N2,)),
-                pltpu.SemaphoreType.REGULAR((3, 4)),
+                pltpu.SemaphoreType.REGULAR((4, 4)),
                 dma((NGC,)), dma((NGC,)),
             ],
             compiler_params=pltpu.CompilerParams(

time: 56 us -> 51.3 us (0.916)
  Pallas kernels: 53.1 us -> 48.3 us
    pallas_call x1, Pallas kernels: 53.1 us -> 48.3 us  [on_device(): pl.pallas_call(functools.partial(kernel, (GX, GY, XL, YL, NGC)), out_shap...]
where the time goes in v3:
time: 51.3 us; the launch traced here: 51.1 us
  Pallas kernels  48.3 us (94%)
  local copies, waits for them, and re-layouts  2.11 us (4%)
  between operations  0.64 us (1%)
    pallas_call x1, Pallas kernels, on_device(): pl.pallas_call(functools.partial(kernel, (GX, GY, XL, YL, NGC)), out_shap...  48.3 us
    unnamed x2, local copies, waits for them, and re-layouts  2.11 us

profile of v3, /device:TPU:1, one launch (start us, length us, event | category | flops | bytes accessed | tf_op | source)
XLA Modules:
  0.0 51.1 jit_solution(9527986296942601767)
XLA Ops:
  0.6 48.3 %shard_map.68 = (f32[4,1024,128]{2,1,0:T(8,128)S(1)}, f32[1024,128]{1,0:T(8,128)S(1)}) custom-call(f32[1024,128]{1,0:T(8,128)} %bitcast.8, f32[2]{0:T(128)} %fsq.1, f32[4,1024,128]{2,1,0:T(8,128)} %bitcast.7, f32[128,32]{1,0:T(8,128)} %bitcast.9, s32[32,32]{1,0:T(8,128)} %depth_h.1), custom_call_target="tpu_custom_call" | custom-call | tf_op jit(solution)/shard_map/pallas_call | solution.py:593
  49.0 1.3 %copy.9 = f32[2,2,32,32,128]{4,3,2,1,0:T(8,128)} copy(f32[2,2,32,32,128]{4,3,2,1,0:T(8,128)S(1)} %bitcast.5) | data formatting | bytes 4194304
  50.3 0.8 %copy.10 = f32[32,32,128]{2,1,0:T(8,128)} copy(f32[32,32,128]{2,1,0:T(8,128)S(1)} %bitcast.6) | data formatting | bytes 1048576

commit v4 on v3

--- a/solution.py
+++ b/solution.py
@@ -153,7 +153,7 @@
             CS.at[e, k, pl.ds(0, 4), :], CR.at[e, 3 - k, pl.ds(0, 4), :], cs_sem.at[e, k], cr_sem.at[e, 3 - k],
             {"gx": gx + (2 * sx - 1), "gy": gy + (2 * sy - 1)})
 
-    FACES = (2, 3, 0, 1)
+    FACES = (0, 1, 2, 3)
     other = lambda face: face ^ 1
 
     def start_all(copies):
@@ -309,6 +309,15 @@
     def compact(c, xx, yy, strided):
         return padded(c, xx - 1, yy, strided)
 
+    for cp in loads[3:]:
+        cp.wait()
+    pl.semaphore_wait(barrier, peers)
+    start_all([layer_copy(0, l, S, face) for l in range(2) for face in (0, 1)])
+    tell(0, 1)
+    for l in range(2):
+        pack_layer(0, l, S)
+        start_all([layer_copy(0, l, S, face) for face in (2, 3)])
+    pack_corners(0, S)
     loads[0].wait()
     loads[1].wait()
     dt = jnp.transpose(jnp.concatenate(
@@ -324,20 +333,12 @@
         IS[side, 4:5, 0:YL] = DP[x:x + 1, :].astype(jnp.float32)
         IS[2 + side, 0:1, 0:4 * XL] = ot[y:y + 1, :]
         IS[2 + side, 1:2, 0:XL] = dt[y:y + 1, :]
-    for cp in loads[2:]:
-        cp.wait()
-    for l in range(2):
-        pack_layer(0, l, S)
-    pack_corners(0, S)
+    loads[2].wait()
     for side in range(2):
         for k in range(XT):
             MYS[side, pl.ds(8 * k, 8), :] = M[pl.ds(8 * k * YL + side * (YL - 1), 8, stride=YL), :]
-    pl.semaphore_wait(barrier, peers)
-    start_all([layer_copy(0, 0, S, face) for face in FACES])
     start_all([info_copy(face) for face in FACES])
-    start_all([layer_copy(0, 1, S, face) for face in FACES])
     start_all([model_copy(face) for face in FACES])
-    tell(0, 1)
 
     lanef = lane.astype(jnp.float32)
     for x in range(XL):
@@ -357,10 +358,10 @@
             acc = acc + v * v
         return tuple(acc if i == f else carry[i] for i in range(2))
 
-    rr = sweep(S, -1.0, finish_b, (zero, zero))
     told(0, 1)
     start_all([corner_copy(0, k) for k in range(4)])
     tell(1, 2)
+    rr = sweep(S, -1.0, finish_b, (zero, zero))
 
     def finish_u(f, o, r, cen, out, carry):
         acc = carry[f]
@@ -408,11 +409,11 @@
     for face in FACES:
         dq = strip(0, S, face, finish_bh, dq)
     pack_corners(1, U)
+    start_all([corner_copy(1, k) for k in range(4)])
+    start_all([layer_copy(1, l, U, face) for l in range(2) for face in (0, 1)])
     for l in range(2):
         pack_layer(1, l, U)
-    start_all([corner_copy(1, k) for k in range(4)])
-    for l in range(2):
-        start_all([layer_copy(1, l, U, face) for face in FACES])
+        start_all([layer_copy(1, l, U, face) for face in (2, 3)])
     told(2, 4)
     tell(3, 8)
 

time: 51.3 us -> 49.2 us (0.959)
  Pallas kernels: 48.3 us -> 46.3 us
    pallas_call x1, Pallas kernels: 48.3 us -> 46.3 us  [on_device(): pl.pallas_call(functools.partial(kernel, (GX, GY, XL, YL, NGC)), out_shap...]
where the time goes in v4:
time: 49.2 us; the launch traced here: 49.1 us
  Pallas kernels  46.3 us (94%)
  local copies, waits for them, and re-layouts  2.11 us (4%)
  between operations  0.64 us (1%)
    pallas_call x1, Pallas kernels, on_device(): pl.pallas_call(functools.partial(kernel, (GX, GY, XL, YL, NGC)), out_shap...  46.3 us
    unnamed x2, local copies, waits for them, and re-layouts  2.11 us

profile of v4, /device:TPU:1, one launch (start us, length us, event | category | flops | bytes accessed | tf_op | source)
XLA Modules:
  0.0 49.1 jit_solution(2814997090283669779)
XLA Ops:
  0.6 46.3 %shard_map.68 = (f32[4,1024,128]{2,1,0:T(8,128)S(1)}, f32[1024,128]{1,0:T(8,128)S(1)}) custom-call(f32[1024,128]{1,0:T(8,128)} %bitcast.8, f32[2]{0:T(128)} %fsq.1, f32[4,1024,128]{2,1,0:T(8,128)} %bitcast.7, f32[128,32]{1,0:T(8,128)} %bitcast.9, s32[32,32]{1,0:T(8,128)} %depth_h.1), custom_call_target="tpu_custom_call" | custom-call | tf_op jit(solution)/shard_map/pallas_call | solution.py:594
  47.0 1.3 %copy.9 = f32[2,2,32,32,128]{4,3,2,1,0:T(8,128)} copy(f32[2,2,32,32,128]{4,3,2,1,0:T(8,128)S(1)} %bitcast.5) | data formatting | bytes 4194304
  48.3 0.8 %copy.10 = f32[32,32,128]{2,1,0:T(8,128)} copy(f32[32,32,128]{2,1,0:T(8,128)S(1)} %bitcast.6) | data formatting | bytes 1048576

commit v5 on v4

--- a/solution.py
+++ b/solution.py
@@ -14,25 +14,16 @@
 
 def kernel(dims, model_h, fsq, src_h, obs_h, depth_h, field_o, grad_o,
            S, B, U, Q, PP, M, W, WO, OB, DP, X1, X2, Y1, Y2, YS, MX, MY, MYS, IS, IR, CS, CR, WH, WOH, BH,
-           A1R, A2R, GS, GR,
+           A1R, GS, GR,
            load_sem, hs_sem, hr_sem, ms_sem, mr_sem, cs_sem, cr_sem,
-           a1s_sem, a1r_sem, a2s_sem, a2r_sem, tok_sem, gs_sem, gr_sem):
+           a1s_sem, a1r_sem, tok_sem, gs_sem, gr_sem):
     GX, GY, XL, YL, NGC = dims
     PX = XL + 2
     NT = YL // 8
     XT = XL // 8
-    N1 = GX * 2
-    N2 = GY // 2
     gx = lax.axis_index("gx")
     gy = lax.axis_index("gy")
     af = lax.axis_index("af")
-
-    def first(j):
-        r = lax.rem(gx * 2 + lax.rem(gy, 2) + j, N1)
-        return r // 2, (gy // 2) * 2 + lax.rem(r, 2)
-
-    def second(j):
-        return lax.rem(gy // 2 + j, N2) * 2 + lax.rem(gy, 2)
 
     def axis_peer(n, sign, axis):
         at, size, name = ((gx, GX, "gx"), (gy, GY, "gy"))[axis]
@@ -362,6 +353,8 @@
     start_all([corner_copy(0, k) for k in range(4)])
     tell(1, 2)
     rr = sweep(S, -1.0, finish_b, (zero, zero))
+    told(1, 2)
+    tell(2, 4)
 
     def finish_u(f, o, r, cen, out, carry):
         acc = carry[f]
@@ -373,8 +366,8 @@
     dq = sweep_inner(B, 1.0, finish_u, (zero, zero))
     arrive_layer(0, 0, S)
     rr = correct(0, B, rr)
-    told(1, 2)
-    tell(2, 4)
+    told(2, 4)
+    tell(3, 8)
     dq = sweep_outer(B, 1.0, finish_u, dq)
 
     arrive_all(info_copy, FACES)
@@ -414,8 +407,9 @@
     for l in range(2):
         pack_layer(1, l, U)
         start_all([layer_copy(1, l, U, face) for face in (2, 3)])
-    told(2, 4)
-    tell(3, 8)
+    told(3, 8)
+    tell(4, 1)
+    tell(5, 4)
 
     def finish_q(f, o, r, cen, out, carry):
         dq, qq = carry[f], carry[2 + f]
@@ -441,10 +435,13 @@
             acc = acc + (out[c] * out[c] + w * (cen[c] * cen[c]))
         return tuple(acc if i == f else carry[i] for i in range(2))
 
+    told(4, 1)
+    told(5, 4)
+    tell(6, 2)
+    tell(7, 8)
     qmq = sweep_inner(Q, 1.0, finish_p, (zero, zero))
     arrive_layer(1, 0, U)
     qq = correct(1, Q, qq)
-    told(3, 8)
     qmq = sweep_outer(Q, 1.0, finish_p, qmq)
 
     def finish_qh(face, k, f, out, carry):
@@ -460,21 +457,28 @@
     arrive_corners(1)
     for face in FACES:
         qmq = strip(1, U, face, finish_qh, qmq)
+    told(6, 2)
+    told(7, 8)
 
     group = lane // 16
 
-    def first_copy(j, slot):
-        px, py = first(j)
+    NALL = GX * GY
+    xs = [lax.rem(gx + a, GX) for a in range(GX)]
+    ys = [lax.rem(gy + a, GY) for a in range(GY)]
+
+    def sum_copy(j):
+        a, b = j // GY, j % GY
+        slot = ((GX - a) % GX) * GY + (GY - b) % GY
         return pltpu.make_async_remote_copy(
             src_ref=A1R.at[pl.ds(0, 1), :], dst_ref=A1R.at[pl.ds(slot, 1), :],
-            send_sem=a1s_sem.at[j], recv_sem=a1r_sem.at[slot],
-            device_id={"gx": px, "gy": py}, device_id_type=MESH)
-
-    def second_copy(j, slot):
+            send_sem=a1s_sem, recv_sem=a1r_sem,
+            device_id={"gx": xs[a], "gy": ys[b]}, device_id_type=MESH)
+
+    def all_copies():
+        rows = A1R.at[pl.ds(1, NALL - 1), :]
         return pltpu.make_async_remote_copy(
-            src_ref=A2R.at[pl.ds(0, 1), :], dst_ref=A2R.at[pl.ds(slot, 1), :],
-            send_sem=a2s_sem.at[j], recv_sem=a2r_sem.at[slot],
-            device_id={"gy": second(j)}, device_id_type=MESH)
+            src_ref=rows, dst_ref=rows, send_sem=a1s_sem, recv_sem=a1r_sem,
+            device_id={"gx": xs[0], "gy": ys[1]}, device_id_type=MESH)
 
     def reduce_first(parts):
         mix = zero
@@ -483,29 +487,18 @@
                 v = v + pltpu.roll(v, shift, 1)
             mix = jnp.where(group == i, v, mix)
         A1R[pl.ds(0, 1), :] = jnp.sum(mix, axis=0, keepdims=True)
-        for j in range(1, N1):
-            first_copy(j, N1 - j).start()
-
-    def reduce_second():
-        for j in range(1, N1):
-            first_copy(j, j).wait_recv()
-        A2R[pl.ds(0, 1), :] = jnp.sum(A1R[...], axis=0, keepdims=True)
-        for j in range(1, N2):
-            second_copy(j, N2 - j).start()
+        for j in range(1, NALL):
+            sum_copy(j).start()
 
     def reduce_end():
-        for j in range(1, N2):
-            second_copy(j, j).wait_recv()
-        v = jnp.broadcast_to(jnp.sum(A2R[...], axis=0, keepdims=True), (8, 128))
+        all_copies().wait_recv()
+        v = jnp.broadcast_to(jnp.sum(A1R[...], axis=0, keepdims=True), (8, 128))
         for shift in (8, 4, 2, 1):
             v = v + pltpu.roll(v, 128 - shift, 1)
         return v
 
     def reduce_drain():
-        for j in range(1, N1):
-            first_copy(j, j).wait_send()
-        for j in range(1, N2):
-            second_copy(j, j).wait_send()
+        all_copies().wait_send()
 
     def row(sums, i):
         return jnp.broadcast_to(sums[:, 16 * i:16 * i + 1], (8, 128))
@@ -517,7 +510,6 @@
         drain_all([corner_copy(e, k) for k in range(4)])
     drain_all([model_copy(face) for face in FACES])
     drain_all([info_copy(face) for face in FACES])
-    reduce_second()
     sums = reduce_end()
 
     cb, cq = [], []
@@ -586,7 +578,6 @@
         XL, YL, ZL = model.shape
         PX = XL + 2
         f32 = jnp.float32
-        N1, N2 = GX * 2, GY // 2
         NGC = 4
         big = pltpu.VMEM((4, PX * YL, ZL), f32)
         col = pltpu.VMEM((XL * YL, ZL), f32)
@@ -623,12 +614,11 @@
                 pltpu.VMEM((4, max(XL, YL), ZL), f32),
                 pltpu.VMEM((4, 4, max(XL, YL), ZL), f32),
                 pltpu.VMEM((4, 4, max(XL, YL), ZL), f32),
-                pltpu.VMEM((N1, ZL), f32),
-                pltpu.VMEM((N2, ZL), f32),
+                pltpu.VMEM((GX * GY, ZL), f32),
                 col, col,
                 dma((7,)), dma((2, 2, 4)), dma((2, 2, 4)), dma((2, 4)), dma((2, 4)), dma((2, 4)), dma((2, 4)),
-                dma((N1,)), dma((N1,)), dma((N2,)), dma((N2,)),
-                pltpu.SemaphoreType.REGULAR((4, 4)),
+                dma(()), dma(()),
+                pltpu.SemaphoreType.REGULAR((8, 4)),
                 dma((NGC,)), dma((NGC,)),
             ],
             compiler_params=pltpu.CompilerParams(

time: 49.2 us -> 47.4 us (0.963)
  Pallas kernels: 46.3 us -> 44.5 us
    pallas_call x1, Pallas kernels: 46.3 us -> 44.5 us  [on_device(): pl.pallas_call(functools.partial(kernel, (GX, GY, XL, YL, NGC)), out_shap...]
where the time goes in v5:
time: 47.4 us; the launch traced here: 47.3 us
  Pallas kernels  44.5 us (94%)
  local copies, waits for them, and re-layouts  2.11 us (4%)
  between operations  0.64 us (1%)
    pallas_call x1, Pallas kernels, on_device(): pl.pallas_call(functools.partial(kernel, (GX, GY, XL, YL, NGC)), out_shap...  44.5 us
    unnamed x2, local copies, waits for them, and re-layouts  2.11 us

profile of v5, /device:TPU:1, one launch (start us, length us, event | category | flops | bytes accessed | tf_op | source)
XLA Modules:
  0.0 47.3 jit_solution(11675339973770196511)
XLA Ops:
  0.6 44.5 %shard_map.68 = (f32[4,1024,128]{2,1,0:T(8,128)S(1)}, f32[1024,128]{1,0:T(8,128)S(1)}) custom-call(f32[1024,128]{1,0:T(8,128)} %bitcast.8, f32[2]{0:T(128)} %fsq.1, f32[4,1024,128]{2,1,0:T(8,128)} %bitcast.7, f32[128,32]{1,0:T(8,128)} %bitcast.9, s32[32,32]{1,0:T(8,128)} %depth_h.1), custom_call_target="tpu_custom_call" | custom-call | tf_op jit(solution)/shard_map/pallas_call | solution.py:585
  45.1 1.3 %copy.9 = f32[2,2,32,32,128]{4,3,2,1,0:T(8,128)} copy(f32[2,2,32,32,128]{4,3,2,1,0:T(8,128)S(1)} %bitcast.5) | data formatting | bytes 4194304
  46.5 0.8 %copy.10 = f32[32,32,128]{2,1,0:T(8,128)} copy(f32[32,32,128]{2,1,0:T(8,128)S(1)} %bitcast.6) | data formatting | bytes 1048576

commit v6 on v5

--- a/solution.py
+++ b/solution.py
@@ -530,9 +530,11 @@
             src_ref=GS.at[pl.ds(g * GROWS, GROWS), :], dst_ref=GR.at[pl.ds(g * GROWS, GROWS), :],
             send_sem=gs_sem.at[g], recv_sem=gr_sem.at[g], device_id={"af": 1 - af}, device_id_type=MESH)
 
+    OUN = 4
+
     def outputs(i, _):
-        for p in range(UN):
-            r0 = pl.multiple_of(i * (UN * YL), 8) + p * YL
+        for p in range(OUN):
+            r0 = pl.multiple_of(i * (OUN * YL), 8) + p * YL
             for t in range(NT):
                 r = r0 + t * 8
                 g = zero
@@ -552,7 +554,7 @@
         return 0
 
     for g in range(NGC):
-        lax.fori_loop(g * (XL // NGC // UN), (g + 1) * (XL // NGC // UN), outputs, 0)
+        lax.fori_loop(g * (XL // NGC // OUN), (g + 1) * (XL // NGC // OUN), outputs, 0)
         grad_copy(g).start()
 
     for g in range(NGC):

time: 47.4 us -> 47.3 us (level)
  no operation moved by 1% of the time
where the time goes in v6:
time: 47.3 us; the launch traced here: 47.2 us
  Pallas kernels  44.4 us (94%)
  local copies, waits for them, and re-layouts  2.11 us (4%)
  between operations  0.64 us (1%)
    pallas_call x1, Pallas kernels, on_device(): pl.pallas_call(functools.partial(kernel, (GX, GY, XL, YL, NGC)), out_shap...  44.4 us
    unnamed x2, local copies, waits for them, and re-layouts  2.11 us

profile of v6, /device:TPU:1, one launch (start us, length us, event | category | flops | bytes accessed | tf_op | source)
XLA Modules:
  0.0 47.2 jit_solution(16946241487614477224)
XLA Ops:
  0.6 44.4 %shard_map.68 = (f32[4,1024,128]{2,1,0:T(8,128)S(1)}, f32[1024,128]{1,0:T(8,128)S(1)}) custom-call(f32[1024,128]{1,0:T(8,128)} %bitcast.8, f32[2]{0:T(128)} %fsq.1, f32[4,1024,128]{2,1,0:T(8,128)} %bitcast.7, f32[128,32]{1,0:T(8,128)} %bitcast.9, s32[32,32]{1,0:T(8,128)} %depth_h.1), custom_call_target="tpu_custom_call" | custom-call | tf_op jit(solution)/shard_map/pallas_call | solution.py:587
  45.1 1.3 %copy.9 = f32[2,2,32,32,128]{4,3,2,1,0:T(8,128)} copy(f32[2,2,32,32,128]{4,3,2,1,0:T(8,128)S(1)} %bitcast.5) | data formatting | bytes 4194304
  46.4 0.8 %copy.10 = f32[32,32,128]{2,1,0:T(8,128)} copy(f32[32,32,128]{2,1,0:T(8,128)S(1)} %bitcast.6) | data formatting | bytes 1048576
